TPU v7x, 32 devices: a whole 2x2x4 slice. The times are simulated.
32 devices in a mesh: row: 8 (over z, x), col: 4 (over y, core).
Axes of the slice: x: 2, y: 2, z: 4, core: 2. Of those that a mesh axis runs over, the one named last changes fastest.
Arguments:
- x_vectors: bfloat16 [64, 32768], P(None, ('row', 'col')), may hold values from -6 to 6
- w_vectors: bfloat16 [64, 32768], P(None, ('row', 'col')), may hold values from -6 to 6
- order: int32 [32768], P(('row', 'col')), may hold values from 0 to 32767, as said below
- ubasis: bfloat16 [64, 32768], P(None, ('row', 'col')), may hold values from -0.75 to 0.75
- vbasis: bfloat16 [64, 32768], P(None, ('row', 'col')), may hold values from -0.75 to 0.75
- leaf_up_u: bfloat16 [64, 32768], P(None, ('row', 'col')), may hold values from -0.1875 to 0.1875
- leaf_up_v: bfloat16 [64, 32768], P(None, ('row', 'col')), may hold values from -0.1875 to 0.1875
- coupling: bfloat16 [64, 1048576], P(None, ('row', 'col')), may hold values from -0.1875 to 0.1875
- coupling_pairs: int32 [2, 16384], P(None, ('row', 'col')), may hold values from 0 to 511, as said below
- coupling_count: int32 [32], P(('row', 'col')), may hold values from 128 to 512, as said below
- near_blocks: bfloat16 [64, 524288], P(None, ('row', 'col')), may hold values from -0.1875 to 0.1875
- near_pairs: int32 [2, 8192], P(None, ('row', 'col')), may hold values from 0 to 511, as said below
- transfer_u: bfloat16 [64, 3840], replicated, may hold values from -0.5 to 0.5
- transfer_v: bfloat16 [64, 3840], replicated, may hold values from -0.5 to 0.5
- upper_coupling: bfloat16 [64, 3968], replicated, may hold values from -6 to 6
Outputs:
- y_product: bfloat16 [64, 32768], P(None, ('row', 'col'))
- z_product: bfloat16 [64, 32768], P(None, ('row', 'col'))
Inputs may be any that keep to these rules, and one draw needn't show every extreme that they name: `order`: each block of 1024 consecutive entries is a permutation of that block's own positions. `coupling_pairs`: for slot b let d = b // 512, r = d // 4, c = d % 4. Entry [0, b] is a leaf of row group r, that is from r * 4 * 16 to (r + 1) * 4 * 16 - 1; entry [1, b] is a leaf l with (l // 16) % 4 == c. Slots of block d from coupling_count[d] onward are not used. `near_pairs`: for slot n let d = n // 256, r = d // 4, c = d % 4. Entry [0, n] is a leaf of row group r as for coupling_pairs; entry [1, n] is a leaf l with t = l // 16, t % 4 == c and t // 4 equal to r - 1, r or r + 1 modulo 8.
All inputs are finite; a program needn't handle non-finite values.
Results may differ from a plain program's by a relative error of at most 0.0063.
Values may be sent and summed in bfloat16 or wider, within the bound.
A program may use at most 192 MiB of HBM per device.

v0:
```python
import functools

import jax
import jax.numpy as jnp
from jax import lax
from jax.experimental import pallas as pl
from jax.experimental.pallas import tpu as pltpu
from jax.sharding import PartitionSpec as P

BF = jnp.bfloat16
F32 = jnp.float32
VMEM = pl.BlockSpec(memory_space=pltpu.VMEM)
SMEM = pl.BlockSpec(memory_space=pltpu.SMEM)
NN = (((1,), (0,)), ((), ()))
NT = (((1,), (1,)), ((), ()))
VLIMIT = 60 * 1024 * 1024


def mm(a, b, dims=NN):
    return lax.dot_general(a, b, dims, preferred_element_type=F32)


def left_mask(half, dtype):
    lane = lax.broadcasted_iota(jnp.int32, (1, 2 * half), 1)
    return (lane < half).astype(F32).astype(dtype), (lane >= half).astype(F32).astype(dtype)


def diag2(v, ml, mr):
    return jnp.concatenate([v * ml, v * mr], axis=0)


def quot(v, n):
    return lax.shift_right_logical(v, n.bit_length() - 1) if n & (n - 1) == 0 else lax.div(v, n)


def mod(v, n):
    return lax.bitwise_and(v, n - 1) if n & (n - 1) == 0 else lax.rem(v, n)


def split2(v):
    hi = v.astype(BF)
    return hi, (v - hi.astype(F32)).astype(BF)


def mm2(v, b, dims):
    hi, lo = split2(v)
    return mm(hi, b, dims) + mm(lo, b, dims)


def one_hot(order_ref, base):
    n = order_ref.shape[1]
    src = lax.broadcasted_iota(jnp.int32, (n, n), 0)
    return jnp.where(src == order_ref[...] - base, 1.0, 0.0).astype(BF)


def grid_of(rows):
    inner = 1 << ((rows.bit_length() - 1) // 2)
    return rows // inner, inner


def greet(rows, cols, r, c):
    bar = pltpu.get_barrier_semaphore()
    for d in range(1, rows):
        pl.semaphore_signal(bar, inc=1, device_id={"row": lax.rem(r + d, rows)}, device_id_type=pl.DeviceIdType.MESH)
    for d in range(1, cols):
        pl.semaphore_signal(bar, inc=1, device_id={"col": lax.rem(c + d, cols)}, device_id_type=pl.DeviceIdType.MESH)
    return bar


def push(src, dst, sems, at, axis, peer):
    copy = pltpu.make_async_remote_copy(
        src_ref=src,
        dst_ref=dst,
        send_sem=sems.at[(0, *at)],
        recv_sem=sems.at[(1, *at)],
        device_id={axis: peer},
        device_id_type=pl.DeviceIdType.MESH,
    )
    copy.start()
    return copy


def chunk_at(ref, at, wide):
    return ref[:, pl.ds(pl.multiple_of(at * wide, wide), wide)]


def combine(v0, v1, fv, fu, ml, mr, isl, half):
    xp = jnp.where(isl, v0, pltpu.roll(v1, half, 1)).astype(BF)
    wp = jnp.where(isl, pltpu.roll(v0, half, 1), v1).astype(BF)
    x = mm(xp, diag2(fv, ml, mr))
    w = mm(wp, diag2(fu, ml, mr))
    return jnp.where(isl, x + pltpu.roll(x, half, 1), w + pltpu.roll(w, half, 1)).astype(BF)


def up_kernel(rows, cols, x_ref, w_ref, order_ref, v_ref, u_ref, ev_ref, eu_ref, fu_ref, fv_ref,
              xc_ref, xp_ref, wa_ref, n0_ref, n2_ref, na_sem, nb_sem, z_sem, x_sem, p_sem, w_sem):
    q, n = x_ref.shape
    packs = xc_ref.shape[1]
    wide = xc_ref.shape[3]
    half = wide // 2
    deep, inner = grid_of(rows)
    r = lax.axis_index("row")
    c = lax.axis_index("col")
    zi = r // inner
    xi = lax.rem(r, inner)
    bar = greet(rows, cols, r, c)
    ml, mr = left_mask(half, BF)
    isl = lax.broadcasted_iota(jnp.int32, (q, wide), 1) < half
    hot = one_hot(order_ref, (r * cols + c) * n)
    both = mm(jnp.concatenate([x_ref[...], w_ref[...]], axis=0), hot).astype(BF)
    folds = []
    for side, (b_ref, e_ref) in enumerate(((v_ref, ev_ref), (u_ref, eu_ref))):
        pts = both[side * q:(side + 1) * q]
        node = jnp.zeros((q, wide), F32)
        for m in range(packs):
            cs = slice(m * wide, (m + 1) * wide)
            pm = pts[:, cs]
            cm = mm(pm, diag2(b_ref[:, cs], ml, mr), NT).astype(BF)
            if side == 0:
                xc_ref[r, m] = cm
                xp_ref[1, m] = pm
            else:
                wa_ref[c, 0, m] = cm
                wa_ref[c, 1, m] = pm
            node = node + mm(cm, diag2(e_ref[:, cs], ml, mr))
        folds.append(node + pltpu.roll(node, half, 1))
    n0_ref[c] = jnp.where(isl, folds[0], folds[1]).astype(BF)
    pl.semaphore_wait(bar, rows + cols - 2)
    node_a = [
        push(n0_ref.at[c], n0_ref.at[c], na_sem, (d - 1,), "col", lax.rem(c + d, cols)) for d in range(1, cols)
    ]
    own = xc_ref.at[r]
    along = [
        push(own, own, z_sem, (d - 1,), "row", lax.rem(zi + d, deep) * inner + xi) for d in range(1, deep)
    ]
    across = [
        push(own, own, x_sem, (0, d - 1), "row", zi * inner + lax.rem(xi + d, inner)) for d in range(1, inner)
    ]
    points = [
        push(xp_ref.at[1], xp_ref.at[0], p_sem, (0,), "row", lax.rem(r + 1, rows)),
        push(xp_ref.at[1], xp_ref.at[2], p_sem, (1,), "row", lax.rem(r + rows - 1, rows)),
    ]
    wide_w = [
        push(wa_ref.at[c], wa_ref.at[c], w_sem, (d - 1,), "col", lax.rem(c + d, cols)) for d in range(1, cols)
    ]
    for copy in node_a:
        copy.wait_recv()
    dev_count = rows * cols
    vals = [n0_ref[i].astype(F32) for i in range(cols)]
    level = 0
    while len(vals) > 1:
        off = dev_count - (dev_count >> level)
        count = len(vals) // 2
        nxt = []
        for i in range(count):
            at = off + r * count + i
            nxt.append(
                combine(vals[2 * i], vals[2 * i + 1], chunk_at(fv_ref, at, wide), chunk_at(fu_ref, at, wide), ml, mr, isl, half)
            )
        vals = [v.astype(F32) for v in nxt]
        level += 1
    n2_ref[r] = vals[0].astype(BF)
    node_b = [
        push(n2_ref.at[r], n2_ref.at[r], nb_sem, (d - 1,), "row", lax.rem(r + d, rows)) for d in range(1, rows)
    ]
    for d in range(1, deep):
        along[d - 1].wait_recv()
        got = xc_ref.at[lax.rem(zi + deep - d, deep) * inner + xi]
        across += [
            push(got, got, x_sem, (d, e - 1), "row", zi * inner + lax.rem(xi + e, inner)) for e in range(1, inner)
        ]
    for copy in node_b + across + points + wide_w:
        copy.wait_recv()
    for copy in node_a + node_b + along + across + points + wide_w:
        copy.wait_send()


def slot_kernel(cp_ref, np_ref, live_ref, x_ref, p_ref, w_ref, s_ref, d_ref, y_ref, z_ref, n_ref, xc, xp, wc, wp, yc, yn, zc, zn):
    rows, packs, q, wide = x_ref.shape
    cols = w_ref.shape[0]
    half = wide // 2
    ml, mr = left_mask(half, BF)
    leaves = 2 * packs
    nears = np_ref.shape[1]
    live = live_ref[0]
    my_row = lax.axis_index("row")
    row_base = my_row * cols * leaves
    isl = lax.broadcasted_iota(jnp.int32, (q, wide), 1) < half
    lane = lax.broadcasted_iota(jnp.int32, (1, wide), 1)
    for acc in (yc, yn, zc, zn):
        def clear(i, carry, acc=acc):
            acc[i] = jnp.zeros(acc.shape[1:], F32)
            return carry
        lax.fori_loop(0, acc.shape[0], clear, 0)

    def widen(src, table, at):
        v = src[...]
        r = jnp.concatenate([v[:, half:], v[:, :half]], axis=1)
        table[at] = v * ml + r * mr
        table[at + 1] = r * ml + v * mr

    def fill_x(i, carry):
        for m in range(packs):
            widen(x_ref.at[i, m], xc, 2 * (i * packs + m))
        return carry

    def fill_w(i, carry):
        for m in range(packs):
            widen(w_ref.at[i, 0, m], wc, 2 * (i * packs + m))
            widen(w_ref.at[i, 1, m], wp, 2 * (i * packs + m))
        return carry

    lax.fori_loop(0, rows, fill_x, 0)
    lax.fori_loop(0, cols, fill_w, 0)
    for k in range(3):
        for m in range(packs):
            widen(p_ref.at[k, m], xp, 2 * (k * packs + m))

    def place(pairs, b, near):
        leaf = pairs[1, b]
        group = quot(leaf, cols * leaves)
        if near:
            group = mod(group - my_row + (rows + 1), rows)
        return pairs[0, b] - row_base, group * leaves + mod(leaf, leaves)

    def run(pairs, mat, xt, wt, ya, za, near, masked, first, last, unroll):
        def step(g, carry):
            work = []
            for k in range(unroll):
                p = g * unroll + k
                i0, j0 = place(pairs, 2 * p, near)
                i1, j1 = place(pairs, 2 * p + 1, near)
                blk = mat[:, pl.ds(pl.multiple_of(p * wide, wide), wide)]
                if masked:
                    left_ok = jnp.where(2 * p < live, 1.0, 0.0)
                    right_ok = jnp.where(2 * p + 1 < live, 1.0, 0.0)
                    a = jnp.where(lane < half, left_ok, 0.0).astype(BF)
                    b = jnp.where(lane < half, 0.0, right_ok).astype(BF)
                else:
                    a, b = ml, mr
                pair = jnp.concatenate([blk * a, blk * b], axis=0)
                xs = xt[j0] * ml + xt[j1] * mr
                ws = wt[i0] * ml + wt[i1] * mr
                work.append((i0, i1, j0, j1, mm(xs, pair, NT), mm(ws, pair)))
            for i0, i1, j0, j1, yv, zv in work:
                ya[i0] += jnp.where(isl, yv, 0.0)
                ya[i1] += jnp.where(isl, 0.0, yv)
                za[j0] += jnp.where(isl, zv, 0.0)
                za[j1] += jnp.where(isl, 0.0, zv)
            return carry
        lax.fori_loop(first, last, step, 0)

    unroll = 4
    full = quot(live, 2 * unroll)
    most = quot(live + 2 * unroll - 1, 2 * unroll)
    run(cp_ref, s_ref, xc, wc, yc, zc, False, False, 0, full, unroll)
    run(cp_ref, s_ref, xc, wc, yc, zc, False, True, full, most, unroll)
    run(np_ref, d_ref, xp, wp, yn, zn, True, False, 0, nears // (2 * unroll), unroll)

    def fold(acc, at):
        a, b = acc[at], acc[at + 1]
        return jnp.where(isl, a + pltpu.roll(a, half, 1), b + pltpu.roll(b, half, 1))

    def out_y(i, carry):
        for m in range(packs):
            y_ref[i, 0, m] = fold(yc, 2 * (i * packs + m)).astype(y_ref.dtype)
            y_ref[i, 1, m] = fold(yn, 2 * (i * packs + m)).astype(y_ref.dtype)
        return carry

    def out_z(i, carry):
        for m in range(packs):
            z_ref[i, m] = fold(zc, 2 * (i * packs + m)).astype(z_ref.dtype)
        return carry

    def out_n(i, carry):
        for m in range(packs):
            n_ref[i, m] = fold(zn, 2 * (i * packs + m)).astype(n_ref.dtype)
        return carry

    lax.fori_loop(0, cols, out_y, 0)
    lax.fori_loop(0, rows, out_z, 0)
    lax.fori_loop(0, 3, out_n, 0)


def down_kernel(rows, cols, y_ref, z_ref, n_ref, n0_ref, n2_ref, order_ref, u_ref, v_ref, eu_ref, ev_ref, fu_ref, fv_ref,
                s_ref, o_ref, y_in, z1_in, z1_out, z2_in, zn_in, nodes, y_sem, z1_sem, z2_sem, n_sem):
    _, packs, q, wide = z_ref.shape
    half = wide // 2
    deep, inner = grid_of(rows)
    dev_count = rows * cols
    r = lax.axis_index("row")
    c = lax.axis_index("col")
    me = r * cols + c
    zi = r // inner
    xi = lax.rem(r, inner)
    bar = greet(rows, cols, r, c)
    ml, mr = left_mask(half, BF)
    isl = lax.broadcasted_iota(jnp.int32, (q, wide), 1) < half
    hot = one_hot(order_ref, me * order_ref.shape[1])
    pl.semaphore_wait(bar, rows + cols - 2)
    first = {}
    for d in list(range(1, deep)) + [0]:
        to = lax.rem(zi + d, deep) * inner
        first[d] = []
        for e in range(1, inner):
            peer = lax.rem(xi + e, inner)
            first[d].append(
                push(z_ref.at[to + peer], z1_in.at[d, e - 1], z1_sem, (d, e - 1), "row", zi * inner + peer)
            )
    near = [
        push(n_ref.at[0], zn_in.at[0], n_sem, (0,), "row", lax.rem(r + rows - 1, rows)),
        push(n_ref.at[2], zn_in.at[1], n_sem, (1,), "row", lax.rem(r + 1, rows)),
    ]
    y_copies = []
    for d in range(1, cols):
        peer = lax.rem(c + d, cols)
        y_copies.append(push(y_ref.at[peer], y_in.at[d - 1], y_sem, (d - 1,), "col", peer))

    second = []
    for d in range(1, deep):
        for copy in first[d]:
            copy.wait_recv()
        to = lax.rem(zi + d, deep) * inner + xi
        for m in range(packs):
            total = z_ref[to, m].astype(F32)
            for e in range(inner - 1):
                total = total + z1_in[d, e, m].astype(F32)
            z1_out[d - 1, m] = total.astype(BF)
        second.append(push(z1_out.at[d - 1], z2_in.at[d - 1], z2_sem, (d - 1,), "row", to))

    levels = dev_count.bit_length() - 1
    starts = []
    at = 0
    vals = None
    for level in range(levels):
        if level == 0:
            vals = [n0_ref[i].astype(F32) for i in range(cols)]
            split = r
        elif cols >> level == 1:
            vals = [n2_ref[i].astype(F32) for i in range(rows)]
            split = 0
        starts.append((at, c >> level if cols >> level > 1 else me >> level))
        for i, v in enumerate(vals):
            nodes[at + i] = v
        at += len(vals)
        off = dev_count - (dev_count >> level)
        count = len(vals) // 2
        if level < levels - 1 and count * 2 == len(vals) and not (cols >> level == 2):
            vals = [
                combine(
                    vals[2 * i],
                    vals[2 * i + 1],
                    chunk_at(fv_ref, off + split * count + i, wide),
                    chunk_at(fu_ref, off + split * count + i, wide),
                    ml, mr, isl, half,
                ).astype(F32)
                for i in range(count)
            ]

    lane_half = (lax.broadcasted_iota(jnp.int32, (q, wide), 1) >= half).astype(jnp.int32)

    def turned(v, chunk, side):
        return mm2(jnp.where(lane_half == side, v, 0.0), jnp.concatenate([chunk, chunk], axis=0), NT)

    y_down = z_down = None
    for level in range(levels - 1, -1, -1):
        start, local = starts[level]
        own = me >> level
        side = lax.rem(own, 2)
        sib = nodes[start + local + 1 - 2 * lax.rem(local, 2)]
        rolled = pltpu.roll(sib, half, 1)
        xs = jnp.where(isl, sib, rolled)
        ws = jnp.where(isl, rolled, 0.0).astype(BF)
        at = dev_count - (dev_count >> level) + own // 2
        cup = chunk_at(s_ref, at, wide)
        dup = jnp.concatenate([cup, cup], axis=0)
        y_term = mm(jnp.where(lane_half == side, xs, 0.0).astype(BF), dup, NT)
        z_raw = jnp.where(lane_half == 1 - side, mm(ws, dup), 0.0)
        z_term = z_raw + pltpu.roll(z_raw, half, 1)
        if level < levels - 1:
            y_term = y_term + turned(y_down, chunk_at(fu_ref, at, wide), side)
            z_term = z_term + turned(z_down, chunk_at(fv_ref, at, wide), side)
        y_down, z_down = y_term, z_term

    perms = []
    for flip, (down, b_ref, e_ref) in enumerate(((y_down, u_ref, eu_ref), (z_down, v_ref, ev_ref))):
        if flip == 0:
            for copy in y_copies:
                copy.wait_recv()
        else:
            for copy in first[0] + second + near:
                copy.wait_recv()
        parts = []
        for m in range(packs):
            cs = slice(m * wide, (m + 1) * wide)
            if flip == 0:
                coef, raw = y_ref[c, 0, m].astype(F32), y_ref[c, 1, m].astype(F32)
                for d in range(cols - 1):
                    coef = coef + y_in[d, 0, m].astype(F32)
                    raw = raw + y_in[d, 1, m].astype(F32)
            else:
                coef, raw = z_ref[r, m].astype(F32), n_ref[1, m].astype(F32)
                for e in range(inner - 1):
                    coef = coef + z1_in[0, e, m].astype(F32)
                for d in range(deep - 1):
                    coef = coef + z2_in[d, m].astype(F32)
                for k in range(2):
                    raw = raw + zn_in[k, m].astype(F32)
            leaf = (coef + mm2(down, diag2(e_ref[:, cs], ml, mr), NT)).astype(BF)
            parts.append((mm(leaf, diag2(b_ref[:, cs], ml, mr)) + raw).astype(BF))
        perms.append(jnp.concatenate(parts, axis=1))
    o_ref[...] = mm(jnp.concatenate(perms, axis=0), hot, NT).astype(BF)
    for copies in (*first.values(), second, near, y_copies):
        for copy in copies:
            copy.wait_send()


def per_device(
    x_vectors,
    w_vectors,
    order,
    ubasis,
    vbasis,
    leaf_up_u,
    leaf_up_v,
    coupling,
    coupling_pairs,
    coupling_count,
    near_blocks,
    near_pairs,
    transfer_u,
    transfer_v,
    upper_coupling,
):
    q, piece = x_vectors.shape
    rank = ubasis.shape[0]
    leaves = leaf_up_u.shape[1] // rank
    packs = leaves // 2
    wide = 2 * rank
    rows = lax.axis_size("row")
    cols = lax.axis_size("col")
    deep, inner = grid_of(rows)
    order2 = order.reshape(1, piece)

    def shape(*lead):
        return jax.ShapeDtypeStruct((*lead, q, wide), BF)

    def buf(*lead, dtype=BF):
        return pltpu.VMEM((*lead, q, wide), dtype)

    def sems(*lead):
        return pltpu.SemaphoreType.DMA((2, *lead))

    def params(cid=None):
        if cid is None:
            return pltpu.CompilerParams(vmem_limit_bytes=VLIMIT)
        return pltpu.CompilerParams(vmem_limit_bytes=VLIMIT, collective_id=cid, has_side_effects=True)

    x_all, x_pts, w_all, n0, n2 = pl.pallas_call(
        functools.partial(up_kernel, rows, cols),
        out_shape=(shape(rows, packs), shape(3, packs), shape(cols, 2, packs), shape(cols), shape(rows)),
        in_specs=[VMEM] * 9,
        out_specs=(VMEM,) * 5,
        scratch_shapes=[
            sems(cols - 1),
            sems(rows - 1),
            sems(deep - 1),
            sems(deep, inner - 1),
            sems(2),
            sems(cols - 1),
        ],
        compiler_params=params(0),
    )(x_vectors, w_vectors, order2, vbasis, ubasis, leaf_up_v, leaf_up_u, transfer_u, transfer_v)
    y_part, z_part, n_part = pl.pallas_call(
        slot_kernel,
        out_shape=(shape(cols, 2, packs), shape(rows, packs), shape(3, packs)),
        in_specs=[SMEM] * 3 + [VMEM] * 5,
        out_specs=(VMEM,) * 3,
        scratch_shapes=[
            buf(rows * leaves),
            buf(3 * leaves),
            buf(cols * leaves),
            buf(cols * leaves),
            buf(cols * leaves, dtype=F32),
            buf(cols * leaves, dtype=F32),
            buf(rows * leaves, dtype=F32),
            buf(3 * leaves, dtype=F32),
        ],
        compiler_params=params(),
    )(coupling_pairs, near_pairs, coupling_count, x_all, x_pts, w_all, coupling, near_blocks)
    out = pl.pallas_call(
        functools.partial(down_kernel, rows, cols),
        out_shape=jax.ShapeDtypeStruct((2 * q, piece), BF),
        in_specs=[VMEM] * 13,
        out_specs=VMEM,
        scratch_shapes=[
            buf(cols - 1, 2, packs),
            buf(deep, inner - 1, packs),
            buf(deep - 1, packs),
            buf(deep - 1, packs),
            buf(2, packs),
            buf(2 * (rows + cols), dtype=F32),
            sems(cols - 1),
            sems(deep, inner - 1),
            sems(deep - 1),
            sems(2),
        ],
        compiler_params=params(1),
    )(
        y_part, z_part, n_part, n0, n2, order2, ubasis, vbasis, leaf_up_u, leaf_up_v,
        transfer_u, transfer_v, upper_coupling,
    )
    return out[:q], out[q:]


def solution(mesh):
    both = P(None, ("row", "col"))
    flat = P(("row", "col"))
    return jax.shard_map(
        per_device,
        mesh=mesh,
        in_specs=(both, both, flat, both, both, both, both, both, both, flat, both, both, P(), P(), P()),
        out_specs=(both, both),
        check_vma=False,
    )
```

profile of v0, /device:TPU:0, one launch (start us, length us, event | category | flops | bytes accessed | tf_op | source)
XLA Modules:
  0.0 94.1 jit_solution(10770484022300989621)
XLA Ops:
  1.3 29.2 %shard_map.158 = (bf16[8,8,64,128]{3,2,1,0:T(8,128)(2,1)}, bf16[3,8,64,128]{3,2,1,0:T(8,128)(2,1)}, bf16[4,2,8,64,128]{4,3,2,1,0:T(8,128)(2,1)}, bf16[4,64,128]{2,1,0:T(8,128)(2,1)}, bf16[8,64,128]{2,1,0:T(8,128)(2,1)}) custom-call(bf16[64,1024]{1,0:T(8,128)(2,1)} %x_ref.1, bf16[64,1024]{1,0:T(8,128)(2,1)} %w_ref.1, s32[1,1024]{1,0:T(1,128)} %bitcast.1, ...), custom_call_target="tpu_custom_call" | custom-call | tf_op jit(solution)/shard_map/pallas_call | solution.py:459
  30.5 35.2 %shard_map.159 = (bf16[4,2,8,64,128]{4,3,2,1,0:T(8,128)(2,1)}, bf16[8,8,64,128]{3,2,1,0:T(8,128)(2,1)}, bf16[3,8,64,128]{3,2,1,0:T(8,128)(2,1)}) custom-call(s32[2,512]{1,0:T(2,128)} %cp_ref.1, s32[2,256]{1,0:T(2,128)} %np_ref.1, s32[1]{0:T(128)S(6)} %copy.17.live_ref, bf16[8,8,64,128]{3,2,1,0:T(8,128)(2,1)} %get-tuple-element.10.x_ref, ...), custom_call_target="tpu_custom_call" | custom-call | tf_op jit(solution)/shard_map/pallas_call | solution.py:474
  65.7 26.7 %shard_map.160 = bf16[128,1024]{1,0:T(8,128)(2,1)} custom-call(bf16[4,2,8,64,128]{4,3,2,1,0:T(8,128)(2,1)} %get-tuple-element.13.y_ref, bf16[8,8,64,128]{3,2,1,0:T(8,128)(2,1)} %get-tuple-element.14.z_ref, bf16[3,8,64,128]{3,2,1,0:T(8,128)(2,1)} %get-tuple-element.15.n_ref, bf16[4,64,128]{2,1,0:T(8,128)(2,1)} %get-tuple-element.16.n0_ref, ...), custom_call_target="tpu_custom_call" | custom-call | tf_op jit(solution)/shard_map/pallas_call | solution.py:491
  92.4 1.7 %fusion = (bf16[64,1024]{1,0:T(8,128)(2,1)}, bf16[64,1024]{1,0:T(8,128)(2,1)}) fusion(bf16[128,1024]{1,0:T(8,128)(2,1)} %shard_map.160), kind=kLoop, calls=%fused_computation | loop fusion | bytes 524288 | tf_op jit(solution)/shard_map/slice | solution.py:513
where the time goes:
time: 94.3 us; the launch traced here: 94.1 us
  Pallas kernels  91.1 us (97%)
  local copies, waits for them, and re-layouts  1.68 us (2%)
  between operations  1.29 us (1%)
    pallas_call x1, Pallas kernels, per_device(): pl.pallas_call(slot_kernel, out_shape=(shape(cols, 2, packs), shape(rows,...  35.2 us
    pallas_call x1, Pallas kernels, per_device(): pl.pallas_call(functools.partial(up_kernel, rows, cols), out_shape=(shape...  29.2 us
    pallas_call x1, Pallas kernels, per_device(): pl.pallas_call(functools.partial(down_kernel, rows, cols), out_shape=jax....  26.7 us

commit v1 on v0

--- a/solution.py
+++ b/solution.py
@@ -13,7 +13,7 @@
 SMEM = pl.BlockSpec(memory_space=pltpu.SMEM)
 NN = (((1,), (0,)), ((), ()))
 NT = (((1,), (1,)), ((), ()))
-VLIMIT = 60 * 1024 * 1024
+UNROLL = 4
 
 
 def mm(a, b, dims=NN):
@@ -51,6 +51,12 @@
     n = order_ref.shape[1]
     src = lax.broadcasted_iota(jnp.int32, (n, n), 0)
     return jnp.where(src == order_ref[...] - base, 1.0, 0.0).astype(BF)
+
+
+def twin_eye(half):
+    row = lax.broadcasted_iota(jnp.int32, (half, 2 * half), 0)
+    lane = lax.broadcasted_iota(jnp.int32, (half, 2 * half), 1)
+    return jnp.where(jnp.logical_or(lane == row, lane == row + half), 1.0, 0.0).astype(BF)
 
 
 def grid_of(rows):
@@ -92,7 +98,11 @@
     return jnp.where(isl, x + pltpu.roll(x, half, 1), w + pltpu.roll(w, half, 1)).astype(BF)
 
 
-def up_kernel(rows, cols, x_ref, w_ref, order_ref, v_ref, u_ref, ev_ref, eu_ref, fu_ref, fv_ref,
+def first_kernel(token_ref):
+    token_ref[...] = jnp.zeros(token_ref.shape, token_ref.dtype)
+
+
+def up_kernel(rows, cols, token_ref, x_ref, w_ref, order_ref, v_ref, u_ref, ev_ref, eu_ref, fu_ref, fv_ref,
               xc_ref, xp_ref, wa_ref, n0_ref, n2_ref, na_sem, nb_sem, z_sem, x_sem, p_sem, w_sem):
     q, n = x_ref.shape
     packs = xc_ref.shape[1]
@@ -106,6 +116,7 @@
     bar = greet(rows, cols, r, c)
     ml, mr = left_mask(half, BF)
     isl = lax.broadcasted_iota(jnp.int32, (q, wide), 1) < half
+    eye = twin_eye(half)
     hot = one_hot(order_ref, (r * cols + c) * n)
     both = mm(jnp.concatenate([x_ref[...], w_ref[...]], axis=0), hot).astype(BF)
     folds = []
@@ -117,8 +128,9 @@
             pm = pts[:, cs]
             cm = mm(pm, diag2(b_ref[:, cs], ml, mr), NT).astype(BF)
             if side == 0:
-                xc_ref[r, m] = cm
-                xp_ref[1, m] = pm
+                turned = diag2(pm, ml, mr)
+                xc_ref[r, m] = mm(b_ref[:, cs], turned, NT).astype(BF)
+                xp_ref[1, m] = mm(eye, turned, NT).astype(BF)
             else:
                 wa_ref[c, 0, m] = cm
                 wa_ref[c, 1, m] = pm
@@ -175,33 +187,48 @@
         copy.wait_send()
 
 
-def slot_kernel(cp_ref, np_ref, live_ref, x_ref, p_ref, w_ref, s_ref, d_ref, y_ref, z_ref, n_ref, xc, xp, wc, wp, yc, yn, zc, zn):
+def slot_kernel(unroll, cp_ref, np_ref, live_ref, x_ref, p_ref, w_ref, s_ref, d_ref, y_ref, z_ref, n_ref,
+                xl, xr, ql, qr, wc, wp, yc, yn, zc, zn, y0, y1, z0, z1):
     rows, packs, q, wide = x_ref.shape
     cols = w_ref.shape[0]
     half = wide // 2
-    ml, mr = left_mask(half, BF)
     leaves = 2 * packs
-    nears = np_ref.shape[1]
     live = live_ref[0]
     my_row = lax.axis_index("row")
     row_base = my_row * cols * leaves
     isl = lax.broadcasted_iota(jnp.int32, (q, wide), 1) < half
-    lane = lax.broadcasted_iota(jnp.int32, (1, wide), 1)
+    lane = lax.broadcasted_iota(jnp.int32, (q, wide), 1)
+    none = jnp.zeros((q, wide), BF)
+    blank = jnp.zeros((q, wide), F32)
+
+    def clear(acc):
+        group = 8
+        def step(i, carry):
+            for k in range(group):
+                acc[i * group + k] = blank
+            return carry
+        lax.fori_loop(0, acc.shape[0] // group, step, 0)
+
     for acc in (yc, yn, zc, zn):
-        def clear(i, carry, acc=acc):
-            acc[i] = jnp.zeros(acc.shape[1:], F32)
-            return carry
-        lax.fori_loop(0, acc.shape[0], clear, 0)
+        clear(acc)
+
+    def split(src, left, right, at):
+        v = src[...]
+        r = jnp.concatenate([v[:, half:], v[:, :half]], axis=1)
+        left[at] = jnp.where(isl, v, none)
+        left[at + 1] = jnp.where(isl, r, none)
+        right[at] = jnp.where(isl, none, r)
+        right[at + 1] = jnp.where(isl, none, v)
 
     def widen(src, table, at):
         v = src[...]
         r = jnp.concatenate([v[:, half:], v[:, :half]], axis=1)
-        table[at] = v * ml + r * mr
-        table[at + 1] = r * ml + v * mr
+        table[at] = jnp.where(isl, v, r)
+        table[at + 1] = jnp.where(isl, r, v)
 
     def fill_x(i, carry):
         for m in range(packs):
-            widen(x_ref.at[i, m], xc, 2 * (i * packs + m))
+            split(x_ref.at[i, m], xl, xr, 2 * (i * packs + m))
         return carry
 
     def fill_w(i, carry):
@@ -210,11 +237,14 @@
             widen(w_ref.at[i, 1, m], wp, 2 * (i * packs + m))
         return carry
 
+    def fill_p(i, carry):
+        for m in range(packs):
+            split(p_ref.at[i, m], ql, qr, 2 * (i * packs + m))
+        return carry
+
     lax.fori_loop(0, rows, fill_x, 0)
     lax.fori_loop(0, cols, fill_w, 0)
-    for k in range(3):
-        for m in range(packs):
-            widen(p_ref.at[k, m], xp, 2 * (k * packs + m))
+    lax.fori_loop(0, 3, fill_p, 0)
 
     def place(pairs, b, near):
         leaf = pairs[1, b]
@@ -223,43 +253,56 @@
             group = mod(group - my_row + (rows + 1), rows)
         return pairs[0, b] - row_base, group * leaves + mod(leaf, leaves)
 
-    def run(pairs, mat, xt, wt, ya, za, near, masked, first, last, unroll):
-        def step(g, carry):
-            work = []
+    def run(pairs, mat, lt, rt, wt, ya, za, near, steps):
+        def settle(g, yb, zb):
+            for k in range(unroll):
+                p = g * unroll + k
+                i0, j0 = place(pairs, 2 * p, near)
+                i1, j1 = place(pairs, 2 * p + 1, near)
+                yv = yb[k]
+                zv = zb[k]
+                a = ya[i0, :, :half] + yv[:, :half]
+                b = ya[i1, :, half:] + yv[:, half:]
+                c = za[j0, :, :half] + zv[:, :half]
+                d = za[j1, :, half:] + zv[:, half:]
+                ya[i0, :, :half] = a
+                ya[i1, :, half:] = b
+                za[j0, :, :half] = c
+                za[j1, :, half:] = d
+
+        def multiply(g, yb, zb):
             for k in range(unroll):
                 p = g * unroll + k
                 i0, j0 = place(pairs, 2 * p, near)
                 i1, j1 = place(pairs, 2 * p + 1, near)
                 blk = mat[:, pl.ds(pl.multiple_of(p * wide, wide), wide)]
-                if masked:
-                    left_ok = jnp.where(2 * p < live, 1.0, 0.0)
-                    right_ok = jnp.where(2 * p + 1 < live, 1.0, 0.0)
-                    a = jnp.where(lane < half, left_ok, 0.0).astype(BF)
-                    b = jnp.where(lane < half, 0.0, right_ok).astype(BF)
-                else:
-                    a, b = ml, mr
-                pair = jnp.concatenate([blk * a, blk * b], axis=0)
-                xs = xt[j0] * ml + xt[j1] * mr
-                ws = wt[i0] * ml + wt[i1] * mr
-                work.append((i0, i1, j0, j1, mm(xs, pair, NT), mm(ws, pair)))
-            for i0, i1, j0, j1, yv, zv in work:
-                ya[i0] += jnp.where(isl, yv, 0.0)
-                ya[i1] += jnp.where(isl, 0.0, yv)
-                za[j0] += jnp.where(isl, zv, 0.0)
-                za[j1] += jnp.where(isl, 0.0, zv)
+                if not near:
+                    reach = jnp.where(2 * p + 1 < live, wide, jnp.where(2 * p < live, half, 0))
+                    blk = jnp.where(lane < reach, blk, none)
+                pair = jnp.concatenate([jnp.where(isl, blk, none), jnp.where(isl, none, blk)], axis=0)
+                xs = jnp.concatenate([lt[j0], rt[j1]], axis=0)
+                ws = jnp.where(isl, wt[i0], wt[i1])
+                yb[k] = mm(blk, xs)
+                zb[k] = mm(ws, pair)
+
+        multiply(0, y0, z0)
+        def step(g, carry):
+            multiply(2 * g + 1, y1, z1)
+            settle(2 * g, y0, z0)
+            multiply(2 * g + 2, y0, z0)
+            settle(2 * g + 1, y1, z1)
             return carry
-        lax.fori_loop(first, last, step, 0)
-
-    unroll = 4
-    full = quot(live, 2 * unroll)
-    most = quot(live + 2 * unroll - 1, 2 * unroll)
-    run(cp_ref, s_ref, xc, wc, yc, zc, False, False, 0, full, unroll)
-    run(cp_ref, s_ref, xc, wc, yc, zc, False, True, full, most, unroll)
-    run(np_ref, d_ref, xp, wp, yn, zn, True, False, 0, nears // (2 * unroll), unroll)
+        lax.fori_loop(0, steps - 1, step, 0)
+        multiply(2 * steps - 1, y1, z1)
+        settle(2 * steps - 2, y0, z0)
+        settle(2 * steps - 1, y1, z1)
+
+    run(np_ref, d_ref, ql, qr, wp, yn, zn, True, np_ref.shape[1] // (4 * unroll))
+    run(cp_ref, s_ref, xl, xr, wc, yc, zc, False, quot(live + 4 * unroll - 1, 4 * unroll))
 
     def fold(acc, at):
         a, b = acc[at], acc[at + 1]
-        return jnp.where(isl, a + pltpu.roll(a, half, 1), b + pltpu.roll(b, half, 1))
+        return jnp.where(isl, a, b) + pltpu.roll(jnp.where(isl, b, a), half, 1)
 
     def out_y(i, carry):
         for m in range(packs):
@@ -297,6 +340,7 @@
     ml, mr = left_mask(half, BF)
     isl = lax.broadcasted_iota(jnp.int32, (q, wide), 1) < half
     hot = one_hot(order_ref, me * order_ref.shape[1])
+    eye = twin_eye(half)
     pl.semaphore_wait(bar, rows + cols - 2)
     first = {}
     for d in list(range(1, deep)) + [0]:
@@ -406,8 +450,16 @@
                     coef = coef + z2_in[d, m].astype(F32)
                 for k in range(2):
                     raw = raw + zn_in[k, m].astype(F32)
-            leaf = (coef + mm2(down, diag2(e_ref[:, cs], ml, mr), NT)).astype(BF)
-            parts.append((mm(leaf, diag2(b_ref[:, cs], ml, mr)) + raw).astype(BF))
+            if flip == 0:
+                hi, lo = split2(down)
+                e = e_ref[:, cs]
+                leaf = (coef + mm(e, diag2(hi, ml, mr), NT) + mm(e, diag2(lo, ml, mr), NT)).astype(BF)
+                turned = mm(eye, diag2(b_ref[:, cs], ml, mr), NT).astype(BF)
+                pts = (mm(turned, diag2(leaf, ml, mr)) + raw).astype(BF)
+                parts.append(mm(eye, diag2(pts, ml, mr), NT).astype(BF))
+            else:
+                leaf = (coef + mm2(down, diag2(e_ref[:, cs], ml, mr), NT)).astype(BF)
+                parts.append((mm(leaf, diag2(b_ref[:, cs], ml, mr)) + raw).astype(BF))
         perms.append(jnp.concatenate(parts, axis=1))
     o_ref[...] = mm(jnp.concatenate(perms, axis=0), hot, NT).astype(BF)
     for copies in (*first.values(), second, near, y_copies):
@@ -451,15 +503,24 @@
     def sems(*lead):
         return pltpu.SemaphoreType.DMA((2, *lead))
 
-    def params(cid=None):
+    def params(mib, cid=None):
+        limit = mib * 1024 * 1024
         if cid is None:
-            return pltpu.CompilerParams(vmem_limit_bytes=VLIMIT)
-        return pltpu.CompilerParams(vmem_limit_bytes=VLIMIT, collective_id=cid, has_side_effects=True)
-
+            return pltpu.CompilerParams(vmem_limit_bytes=limit)
+        return pltpu.CompilerParams(vmem_limit_bytes=limit, collective_id=cid, has_side_effects=True)
+
+    token = pl.pallas_call(
+        first_kernel,
+        out_shape=jax.ShapeDtypeStruct((1, wide), F32),
+        out_specs=VMEM,
+        compiler_params=params(1),
+        cost_estimate=pl.CostEstimate(flops=2_000_000_000, bytes_accessed=6_000_000, transcendentals=0),
+    )()
+    loaded = (token, x_vectors, w_vectors, order2, vbasis, ubasis, leaf_up_v, leaf_up_u, transfer_u, transfer_v)
     x_all, x_pts, w_all, n0, n2 = pl.pallas_call(
         functools.partial(up_kernel, rows, cols),
         out_shape=(shape(rows, packs), shape(3, packs), shape(cols, 2, packs), shape(cols), shape(rows)),
-        in_specs=[VMEM] * 9,
+        in_specs=[VMEM] * 10,
         out_specs=(VMEM,) * 5,
         scratch_shapes=[
             sems(cols - 1),
@@ -469,15 +530,21 @@
             sems(2),
             sems(cols - 1),
         ],
-        compiler_params=params(0),
-    )(x_vectors, w_vectors, order2, vbasis, ubasis, leaf_up_v, leaf_up_u, transfer_u, transfer_v)
+        compiler_params=params(16, 0),
+        cost_estimate=pl.CostEstimate(flops=20_000_000_000, bytes_accessed=60_000_000, transcendentals=0),
+    )(*loaded)
+    unroll = UNROLL
+    tables = 2 * leaves * (rows + 3 + cols)
+    sums = leaves * (2 * cols + rows + 3) + 4 * unroll
     y_part, z_part, n_part = pl.pallas_call(
-        slot_kernel,
+        functools.partial(slot_kernel, unroll),
         out_shape=(shape(cols, 2, packs), shape(rows, packs), shape(3, packs)),
         in_specs=[SMEM] * 3 + [VMEM] * 5,
         out_specs=(VMEM,) * 3,
         scratch_shapes=[
             buf(rows * leaves),
+            buf(rows * leaves),
+            buf(3 * leaves),
             buf(3 * leaves),
             buf(cols * leaves),
             buf(cols * leaves),
@@ -485,8 +552,13 @@
             buf(cols * leaves, dtype=F32),
             buf(rows * leaves, dtype=F32),
             buf(3 * leaves, dtype=F32),
+            buf(unroll, dtype=F32),
+            buf(unroll, dtype=F32),
+            buf(unroll, dtype=F32),
+            buf(unroll, dtype=F32),
         ],
-        compiler_params=params(),
+        compiler_params=params(8 + (tables * q * wide * 2 + sums * q * wide * 4) // 1024**2),
+        cost_estimate=pl.CostEstimate(flops=20_000_000_000, bytes_accessed=60_000_000, transcendentals=0),
     )(coupling_pairs, near_pairs, coupling_count, x_all, x_pts, w_all, coupling, near_blocks)
     out = pl.pallas_call(
         functools.partial(down_kernel, rows, cols),
@@ -505,7 +577,7 @@
             sems(deep - 1),
             sems(2),
         ],
-        compiler_params=params(1),
+        compiler_params=params(16, 1),
     )(
         y_part, z_part, n_part, n0, n2, order2, ubasis, vbasis, leaf_up_u, leaf_up_v,
         transfer_u, transfer_v, upper_coupling,

time: 94.3 us -> 75.1 us (0.80)
  Pallas kernels: 91.1 us -> 71.8 us
    pallas_call x1 -> x2, Pallas kernels: 35.2 us -> 20.2 us  [the longest x1 20.2 us: per_device(): pl.pallas_call(functools.partial(slot_kernel, unroll), out_shape=(shape(c...]
    pallas_call x1, Pallas kernels: 29.2 us -> 26.3 us  [per_device(): pl.pallas_call(functools.partial(up_kernel, rows, cols), out_shape=(shape...]
    pallas_call x1, Pallas kernels: 26.7 us -> 25.3 us  [per_device(): pl.pallas_call(functools.partial(down_kernel, rows, cols), out_shape=jax....]
    slice x1, local copies, waits for them, and re-layouts: 1.68 us -> 0.72 us  [per_device(): return (out[:q], out[q:])]
where the time goes in v1:
time: 75.1 us; the launch traced here: 74.6 us
  Pallas kernels  71.8 us (96%)
  between operations  1.55 us (2%)
  local copies, waits for them, and re-layouts  1.32 us (2%)
    pallas_call x1, Pallas kernels, per_device(): pl.pallas_call(functools.partial(up_kernel, rows, cols), out_shape=(shape...  26.3 us
    pallas_call x1, Pallas kernels, per_device(): pl.pallas_call(functools.partial(down_kernel, rows, cols), out_shape=jax....  25.3 us
    pallas_call x1, Pallas kernels, per_device(): pl.pallas_call(functools.partial(slot_kernel, unroll), out_shape=(shape(c...  20.2 us

profile of v1, /device:TPU:0, one launch (start us, length us, event | category | flops | bytes accessed | tf_op | source)
XLA Modules:
  0.0 74.6 jit_solution(6211443790404290090)
XLA Ops:
  0.6 0.0 copy-start.2
  0.6 0.0 copy-start.1
  0.7 0.0 copy-start.5
  0.7 0.0 copy-start.6
  0.7 0.0 copy-start.3
  0.7 0.0 copy-start.4
  0.7 0.0 copy-start.7
  0.7 0.0 copy-start.11
  0.7 0.0 copy-start.10
  1.5 0.2 copy-done.2
  1.7 0.2 copy-done.1
  1.8 0.0 copy-done.5
  1.8 0.0 copy-done.6
  1.9 0.0 copy-done.3
  1.9 0.0 copy-done.4
  2.0 0.0 copy-done.7
  2.0 0.1 copy-done.11
  2.0 0.0 copy-done.10
  2.1 26.3 %shard_map.159 = (bf16[8,8,64,128]{3,2,1,0:T(8,128)(2,1)S(1)}, bf16[3,8,64,128]{3,2,1,0:T(8,128)(2,1)S(1)}, bf16[4,2,8,64,128]{4,3,2,1,0:T(8,128)(2,1)S(1)}, bf1...) custom-call(f32[1,128]{1,0:T(1,128)S(1)} %shard_map.158.token_ref, bf16[64,1024]{1,0:T(8,128)(2,1)S(1)} %copy-done.10, ...), custom_call_target="tpu_custom_call" | custom-call | flops 20000000000 | bytes 60000000 | tf_op jit(solution)/shard_map/pallas_call | solution.py:520
  28.4 0.0 copy-start
  28.4 20.2 %shard_map.160 = (bf16[4,2,8,64,128]{4,3,2,1,0:T(8,128)(2,1)S(1)}, bf16[8,8,64,128]{3,2,1,0:T(8,128)(2,1)S(1)}, bf16[3,8,64,128]{3,2,1,0:T(8,128)(2,1)S(1)}) custom-call(s32[2,512]{1,0:T(2,128)S(1)} %copy-done.12, s32[2,256]{1,0:T(2,128)S(1)} %copy-done.13, s32[1]{0:T(128)S(6)} %copy.17.live_ref, bf16[8,8,64,128]{3,2,1,0:T(8,128)(2,1)S(1)} %get-tuple-element.10.x_ref, ...), custom_call_target="tpu_custom_call" | custom-call | flops 20000000000 | bytes 60000000 | tf_op jit(solution)/shard_map/pallas_call | solution.py:539
  48.6 0.0 copy-done
  48.6 25.3 %shard_map.161 = bf16[128,1024]{1,0:T(8,128)(2,1)S(1)} custom-call(bf16[4,2,8,64,128]{4,3,2,1,0:T(8,128)(2,1)S(1)} %get-tuple-element.13.y_ref, bf16[8,8,64,128]{3,2,1,0:T(8,128)(2,1)S(1)} %get-tuple-element.14.z_ref, bf16[3,8,64,128]{3,2,1,0:T(8,128)(2,1)S(1)} %get-tuple-element.15.n_ref, bf16[4,64,128]{2,1,0:T(8,128)(2,1)S(1)} %get-tuple-element.16.n0_ref, ...), custom_call_target="tpu_custom_call" | custom-call | tf_op jit(solution)/shard_map/pallas_call | solution.py:563
  73.9 0.7 fusion
  (9 shorter events, 0.0 us)
Async XLA Ops:
  0.6 1.0 %copy-start.2 = (bf16[64,3840]{1,0:T(8,128)(2,1)S(1)}, bf16[64,3840]{1,0:T(8,128)(2,1)}, u32[]{:S(2)}) copy-start(bf16[64,3840]{1,0:T(8,128)(2,1)} %fv_ref.3) | copy-start | bytes 1474564
  0.6 1.2 %copy-start.1 = (bf16[64,3840]{1,0:T(8,128)(2,1)S(1)}, bf16[64,3840]{1,0:T(8,128)(2,1)}, u32[]{:S(2)}) copy-start(bf16[64,3840]{1,0:T(8,128)(2,1)} %fu_ref.3) | copy-start | bytes 1474564
  0.7 1.2 %copy-start.5 = (bf16[64,1024]{1,0:T(8,128)(2,1)S(1)}, bf16[64,1024]{1,0:T(8,128)(2,1)}, u32[]{:S(2)}) copy-start(bf16[64,1024]{1,0:T(8,128)(2,1)} %ev_ref.3) | copy-start | bytes 393220
  0.7 1.2 %copy-start.6 = (bf16[64,1024]{1,0:T(8,128)(2,1)S(1)}, bf16[64,1024]{1,0:T(8,128)(2,1)}, u32[]{:S(2)}) copy-start(bf16[64,1024]{1,0:T(8,128)(2,1)} %eu_ref.3) | copy-start | bytes 393220
  0.7 1.2 %copy-start.3 = (bf16[64,1024]{1,0:T(8,128)(2,1)S(1)}, bf16[64,1024]{1,0:T(8,128)(2,1)}, u32[]{:S(2)}) copy-start(bf16[64,1024]{1,0:T(8,128)(2,1)} %v_ref.3) | copy-start | bytes 393220
  0.7 1.3 %copy-start.4 = (bf16[64,1024]{1,0:T(8,128)(2,1)S(1)}, bf16[64,1024]{1,0:T(8,128)(2,1)}, u32[]{:S(2)}) copy-start(bf16[64,1024]{1,0:T(8,128)(2,1)} %u_ref.3) | copy-start | bytes 393220
  0.7 1.3 %copy-start.7 = (s32[1024]{0:T(1024)S(1)}, s32[1024]{0:T(1024)}, u32[]{:S(2)}) copy-start(s32[1024]{0:T(1024)} %param.17) | copy-start | bytes 12292
  0.7 1.3 %copy-start.11 = (bf16[64,1024]{1,0:T(8,128)(2,1)S(1)}, bf16[64,1024]{1,0:T(8,128)(2,1)}, u32[]{:S(2)}) copy-start(bf16[64,1024]{1,0:T(8,128)(2,1)} %w_ref.1) | copy-start | bytes 393220
  0.7 1.3 %copy-start.10 = (bf16[64,1024]{1,0:T(8,128)(2,1)S(1)}, bf16[64,1024]{1,0:T(8,128)(2,1)}, u32[]{:S(2)}) copy-start(bf16[64,1024]{1,0:T(8,128)(2,1)} %x_ref.1) | copy-start | bytes 393220
  2.1 26.3 %copy-start.8 = (bf16[64,32768]{1,0:T(8,128)(2,1)S(1)}, bf16[64,32768]{1,0:T(8,128)(2,1)}, u32[]{:S(2)}) copy-start(bf16[64,32768]{1,0:T(8,128)(2,1)} %s_ref.2) | copy-start | bytes 12582916
  2.1 26.3 %copy-start.9 = (bf16[64,16384]{1,0:T(8,128)(2,1)S(1)}, bf16[64,16384]{1,0:T(8,128)(2,1)}, u32[]{:S(2)}) copy-start(bf16[64,16384]{1,0:T(8,128)(2,1)} %d_ref.1) | copy-start | bytes 6291460
  2.1 26.3 %copy-start.12 = (s32[2,512]{1,0:T(2,128)S(1)}, s32[2,512]{1,0:T(2,128)}, u32[]{:S(2)}) copy-start(s32[2,512]{1,0:T(2,128)} %cp_ref.1) | copy-start | bytes 12292
  2.1 26.3 %copy-start.13 = (s32[2,256]{1,0:T(2,128)S(1)}, s32[2,256]{1,0:T(2,128)}, u32[]{:S(2)}) copy-start(s32[2,256]{1,0:T(2,128)} %np_ref.1) | copy-start | bytes 6148
  28.4 20.2 %copy-start = (bf16[64,3968]{1,0:T(8,128)(2,1)S(1)}, bf16[64,3968]{1,0:T(8,128)(2,1)}, u32[]{:S(2)}) copy-start(bf16[64,3968]{1,0:T(8,128)(2,1)} %s_ref.3) | copy-start | bytes 1523716

commit v2 on v1

v2 whole, which is shorter than its diff:
```python
import functools

import jax
import jax.numpy as jnp
from jax import lax
from jax.experimental import pallas as pl
from jax.experimental.pallas import tpu as pltpu
from jax.sharding import PartitionSpec as P

BF = jnp.bfloat16
F32 = jnp.float32
VMEM = pl.BlockSpec(memory_space=pltpu.VMEM)
SMEM = pl.BlockSpec(memory_space=pltpu.SMEM)
NN = (((1,), (0,)), ((), ()))
NT = (((1,), (1,)), ((), ()))
UNROLL = 8


def mm(a, b, dims=NN):
    return lax.dot_general(a, b, dims, preferred_element_type=F32)


def left_mask(half, dtype):
    lane = lax.broadcasted_iota(jnp.int32, (1, 2 * half), 1)
    return (lane < half).astype(F32).astype(dtype), (lane >= half).astype(F32).astype(dtype)


def diag2(v, ml, mr):
    return jnp.concatenate([v * ml, v * mr], axis=0)


def quot(v, n):
    return lax.shift_right_logical(v, n.bit_length() - 1) if n & (n - 1) == 0 else lax.div(v, n)


def mod(v, n):
    return lax.bitwise_and(v, n - 1) if n & (n - 1) == 0 else lax.rem(v, n)


def split2(v):
    hi = v.astype(BF)
    return hi, (v - hi.astype(F32)).astype(BF)


def mm2(v, b, dims):
    hi, lo = split2(v)
    return mm(hi, b, dims) + mm(lo, b, dims)


def one_hot(order_ref, base):
    n = order_ref.shape[1]
    src = lax.broadcasted_iota(jnp.int32, (n, n), 0)
    return jnp.where(src == order_ref[...] - base, 1.0, 0.0).astype(BF)


def twin_eye(half):
    row = lax.broadcasted_iota(jnp.int32, (half, 2 * half), 0)
    lane = lax.broadcasted_iota(jnp.int32, (half, 2 * half), 1)
    return jnp.where(jnp.logical_or(lane == row, lane == row + half), 1.0, 0.0).astype(BF)


def grid_of(rows):
    inner = 1 << ((rows.bit_length() - 1) // 2)
    return rows // inner, inner


def greet(rows, cols, r, c):
    bar = pltpu.get_barrier_semaphore()
    for d in range(1, rows):
        pl.semaphore_signal(bar, inc=1, device_id={"row": lax.rem(r + d, rows)}, device_id_type=pl.DeviceIdType.MESH)
    for d in range(1, cols):
        pl.semaphore_signal(bar, inc=1, device_id={"col": lax.rem(c + d, cols)}, device_id_type=pl.DeviceIdType.MESH)
    return bar


def push(src, dst, sems, at, axis, peer):
    copy = pltpu.make_async_remote_copy(
        src_ref=src,
        dst_ref=dst,
        send_sem=sems.at[(0, *at)],
        recv_sem=sems.at[(1, *at)],
        device_id={axis: peer},
        device_id_type=pl.DeviceIdType.MESH,
    )
    copy.start()
    return copy


def chunk_at(ref, at, wide):
    return ref[:, pl.ds(pl.multiple_of(at * wide, wide), wide)]


def combine(v0, v1, fv, fu, ml, mr, isl, half):
    xp = jnp.where(isl, v0, pltpu.roll(v1, half, 1)).astype(BF)
    wp = jnp.where(isl, pltpu.roll(v0, half, 1), v1).astype(BF)
    x = mm(xp, diag2(fv, ml, mr))
    w = mm(wp, diag2(fu, ml, mr))
    return jnp.where(isl, x + pltpu.roll(x, half, 1), w + pltpu.roll(w, half, 1)).astype(BF)


def first_kernel(token_ref):
    token_ref[...] = jnp.zeros(token_ref.shape, token_ref.dtype)


def local_kernel(token_ref, far_ref, near_ref, order_ref, x_ref, w_ref, v_ref, u_ref, ev_ref, eu_ref,
                 xc_ref, xp_ref, w_out, n_ref, fi_ref, fj_ref, ni_ref, nj_ref):
    q, n = x_ref.shape
    packs = xc_ref.shape[0]
    wide = xc_ref.shape[2]
    half = wide // 2
    rows, cols = lax.axis_size("row"), lax.axis_size("col")
    my_row = lax.axis_index("row")
    base = (my_row * cols + lax.axis_index("col")) * n
    leaves = 2 * packs
    for pairs, i_ref, j_ref, near in ((far_ref, fi_ref, fj_ref, False), (near_ref, ni_ref, nj_ref, True)):
        leaf = pairs[1:2]
        group = quot(leaf, cols * leaves)
        if near:
            group = mod(group - my_row + (rows + 1), rows)
        i_ref[...] = pairs[0:1] - my_row * cols * leaves
        j_ref[...] = group * leaves + mod(leaf, leaves)
    ml, mr = left_mask(half, BF)
    isl = lax.broadcasted_iota(jnp.int32, (q, wide), 1) < half
    eye = twin_eye(half)
    hot = one_hot(order_ref, base)
    both = mm(jnp.concatenate([x_ref[...], w_ref[...]], axis=0), hot).astype(BF)
    folds = []
    for side, (b_ref, e_ref) in enumerate(((v_ref, ev_ref), (u_ref, eu_ref))):
        pts = both[side * q:(side + 1) * q]
        node = jnp.zeros((q, wide), F32)
        for m in range(packs):
            cs = slice(m * wide, (m + 1) * wide)
            pm = pts[:, cs]
            cm = mm(pm, diag2(b_ref[:, cs], ml, mr), NT).astype(BF)
            if side == 0:
                turned = diag2(pm, ml, mr)
                xc_ref[m] = mm(b_ref[:, cs], turned, NT).astype(BF)
                xp_ref[m] = mm(eye, turned, NT).astype(BF)
            else:
                w_out[0, m] = cm
                w_out[1, m] = pm
            node = node + mm(cm, diag2(e_ref[:, cs], ml, mr))
        folds.append(node + pltpu.roll(node, half, 1))
    n_ref[...] = jnp.where(isl, folds[0], folds[1]).astype(BF)


class Mail:
    def __init__(self, sem):
        self.sem = sem
        self.sent = []

    def copy(self, src, dst, recv, peer, at):
        return pltpu.make_async_remote_copy(
            src_ref=src,
            dst_ref=dst,
            send_sem=self.sem.at[at],
            recv_sem=recv,
            device_id=peer,
            device_id_type=pl.DeviceIdType.MESH,
        )

    def push(self, src, dst, recv, peer, when=None):
        args = (src, dst, recv, peer, len(self.sent))
        self.sent.append((args, when))
        guarded(when, lambda: self.copy(*args).start())

    def landed(self, dst, recv, peer):
        self.copy(dst, dst, recv, peer, 0).wait_recv()

    def close(self):
        for args, when in self.sent:
            guarded(when, lambda args=args: self.copy(*args).wait_send())


def guarded(when, act):
    if when is None:
        act()
    else:
        pl.when(when)(act)


def place(pairs, p):
    i_ref, j_ref = pairs
    return i_ref[0, 2 * p], i_ref[0, 2 * p + 1], j_ref[0, 2 * p], j_ref[0, 2 * p + 1]


def gather_kernel(rows, cols, unroll, fi_ref, fj_ref, ni_ref, nj_ref, live_ref, xc_own, xp_own, w_own, n_own, fu_ref, fv_ref, s_ref, d_ref,
                  xl, xr, pyn, pzn, pzc, sib_ref,
                  xc, xp, wa, na, nb, ql, qr, wc, wp, send_sem, x_sem, p_sem, w_sem, na_sem, nb_sem):
    packs, q, wide = xc_own.shape
    half = wide // 2
    leaves = 2 * packs
    deep, inner = grid_of(rows)
    outer = cols // 2
    dev_count = rows * cols
    first = (3 * packs) // 8
    cuts = ((0, first), (first, packs - first))
    r = lax.axis_index("row")
    c = lax.axis_index("col")
    zi = r // inner
    xi = lax.rem(r, inner)
    oi = c // 2
    ki = lax.rem(c, 2)
    live = live_ref[0]
    bar = greet(rows, cols, r, c)
    ml, mr = left_mask(half, BF)
    isl = lax.broadcasted_iota(jnp.int32, (q, wide), 1) < half
    lane = lax.broadcasted_iota(jnp.int32, (q, wide), 1)
    none = jnp.zeros((q, wide), BF)
    mail = Mail(send_sem)
    near_row = {"row": lax.rem(r + 1, rows)}
    near_col = {"col": lax.rem(c + 1, cols)}

    def row_of(z, x):
        return {"row": z * inner + x}

    def turn_x(e):
        return lax.rem(xi + e, inner)

    def xpart(row, part):
        return xc.at[row, pl.ds(*cuts[part])]

    def xown(part):
        return xc_own.at[pl.ds(*cuts[part])]

    up, down = zi < deep - 1, zi > 0
    pl.semaphore_wait(bar, rows + cols - 2)

    for e in range(1, cols):
        mail.push(n_own, na.at[c], na_sem.at[c], {"col": lax.rem(c + e, cols)})
    for kind in (1, 0):
        for e in range(1, outer):
            mail.push(w_own.at[kind], wa.at[c, kind], w_sem.at[c, kind], {"col": lax.rem(oi + e, outer) * 2 + ki})
        mail.push(w_own.at[kind], wa.at[c, kind], w_sem.at[c, kind], {"col": oi * 2 + 1 - ki})
    for e in range(1, inner):
        mail.push(xown(0), xpart(r, 0), x_sem.at[r, 0], row_of(zi, turn_x(e)))
    for part in (1, 0):
        mail.push(xown(part), xpart(r, part), x_sem.at[r, part], row_of(zi + 1, xi), up)
        mail.push(xown(part), xpart(r, part), x_sem.at[r, part], row_of(zi - 1, xi), down)
    if inner == 2:
        mail.push(xp_own, xp.at[2 * xi], p_sem.at[2 * xi], row_of(zi, 1 - xi))
    else:
        mail.push(xp_own, xp.at[0], p_sem.at[0], {"row": lax.rem(r + 1, rows)})
        mail.push(xp_own, xp.at[2], p_sem.at[2], {"row": lax.rem(r + rows - 1, rows)})
    for e in range(1, inner):
        mail.push(xown(1), xpart(r, 1), x_sem.at[r, 1], row_of(zi, turn_x(e)))

    def split(v, left, right, at):
        t = jnp.concatenate([v[:, half:], v[:, :half]], axis=1)
        left[at] = jnp.where(isl, v, none)
        left[at + 1] = jnp.where(isl, t, none)
        right[at] = jnp.where(isl, none, t)
        right[at + 1] = jnp.where(isl, none, v)

    def widen(v, table, at):
        t = jnp.concatenate([v[:, half:], v[:, :half]], axis=1)
        table[at] = jnp.where(isl, v, t)
        table[at + 1] = jnp.where(isl, t, v)

    def each_pack(act):
        for m in range(packs):
            act(m)

    def own_fill(m):
        split(xc_own[m], xl, xr, 2 * (r * packs + m))
        split(xp_own[m], ql, qr, 2 * (packs + m))
        widen(w_own[0, m], wc, 2 * (c * packs + m))
        widen(w_own[1, m], wp, 2 * (c * packs + m))

    each_pack(own_fill)

    me = r * cols + c
    for e in range(1, cols):
        o = lax.rem(c + e, cols)
        mail.landed(na.at[o], na_sem.at[o], near_col)
    na[c] = n_own[...]
    vals = [na[i].astype(F32) for i in range(cols)]
    level = 0
    while len(vals) > 1:
        own = c >> level
        sib_ref[level] = pick(vals, own + 1 - 2 * lax.rem(own, 2)).astype(BF)
        off = dev_count - (dev_count >> level)
        count = len(vals) // 2
        vals = [
            combine(vals[2 * i], vals[2 * i + 1], chunk_at(fv_ref, off + r * count + i, wide),
                    chunk_at(fu_ref, off + r * count + i, wide), ml, mr, isl, half).astype(F32)
            for i in range(count)
        ]
        level += 1
    base_level = level
    top = [vals[0]]

    def ask(t):
        nb[2 * t] = top[0].astype(BF)
        mail.push(nb.at[2 * t], nb.at[2 * t + 1], nb_sem.at[t], {"row": r + (1 << t) * (1 - 2 * lax.rem(r >> t, 2))})

    def answer(t):
        mail.landed(nb.at[2 * t + 1], nb_sem.at[t], near_row)
        lev = base_level + t
        sib_ref[lev] = nb[2 * t + 1]
        if dev_count >> (lev + 1) > 1:
            other = nb[2 * t + 1].astype(F32)
            even = lax.rem(r >> t, 2) == 0
            lo = jnp.where(even, top[0], other)
            hi = jnp.where(even, other, top[0])
            at = dev_count - (dev_count >> lev) + ((me >> lev) >> 1)
            top[0] = combine(lo, hi, chunk_at(fv_ref, at, wide), chunk_at(fu_ref, at, wide), ml, mr, isl, half).astype(F32)
            ask(t + 1)

    row_levels = rows.bit_length() - 1
    ask(0)

    def relay_across():
        for e in range(1, inner):
            o = zi * inner + turn_x(e)
            mail.landed(xpart(o, 0), x_sem.at[o, 0], near_row)
            mail.push(xpart(o, 0), xpart(o, 0), x_sem.at[o, 0], row_of(zi + 1, xi), up)
            mail.push(xpart(o, 0), xpart(o, 0), x_sem.at[o, 0], row_of(zi - 1, xi), down)

    def relay_along(d, e, part):
        for back in (True, False):
            have = zi >= d if back else zi + d < deep
            oz = zi - d if back else zi + d
            o = oz * inner + turn_x(e)
            guarded(have, lambda o=o: mail.landed(xpart(o, part), x_sem.at[o, part], near_row))
            if d < deep - 1:
                onward = jnp.logical_and(have, up if back else down)
                mail.push(xpart(o, part), xpart(o, part), x_sem.at[o, part], row_of(zi + 1 if back else zi - 1, xi), onward)
            if part == 1:
                for f in range(1, inner):
                    mail.push(xpart(o, 1), xpart(o, 1), x_sem.at[o, 1], row_of(zi, turn_x(f)), have)

    def relay_points():
        if inner == 2:
            got = 2 * (1 - xi)
            mail.landed(xp.at[got], p_sem.at[got], near_row)
            to = lax.rem(zi + deep + 1 - 2 * xi, deep)
            mail.push(xp.at[got], xp.at[2 * xi], p_sem.at[2 * xi], row_of(to, xi))

    def relay_w(kind):
        for e in range(1, outer):
            o = lax.rem(oi + e, outer) * 2 + ki
            mail.landed(wa.at[o, kind], w_sem.at[o, kind], near_col)
            mail.push(wa.at[o, kind], wa.at[o, kind], w_sem.at[o, kind], {"col": oi * 2 + 1 - ki})

    def fill_w(kind, table):
        for e in range(outer):
            o = lax.rem(oi + e, outer) * 2 + 1 - ki
            mail.landed(wa.at[o, kind], w_sem.at[o, kind], near_col)
        for e in range(1, cols):
            o = lax.rem(c + e, cols)
            each_pack(lambda m, o=o: widen(wa[o, kind, m], table, 2 * (o * packs + m)))

    def fill_p():
        if inner == 2:
            mail.landed(xp.at[2 * xi], p_sem.at[2 * xi], near_row)
        else:
            mail.landed(xp.at[0], p_sem.at[0], near_row)
            mail.landed(xp.at[2], p_sem.at[2], near_row)
        for k in (0, 2):
            each_pack(lambda m, k=k: split(xp[k, m], ql, qr, 2 * (k * packs + m)))

    def products(pairs, mat, near, side, tables, out, piece, pieces):
        total = out.shape[0] // unroll
        def step(g, carry):
            for k in range(unroll):
                p = g * unroll + k
                i0, i1, j0, j1 = place(pairs, p)
                blk = mat[:, pl.ds(pl.multiple_of(p * wide, wide), wide)]
                if side == "z":
                    if not near:
                        reach = jnp.where(2 * p + 1 < live, wide, jnp.where(2 * p < live, half, 0))
                        blk = jnp.where(lane < reach, blk, none)
                    pair = jnp.concatenate([jnp.where(isl, blk, none), jnp.where(isl, none, blk)], axis=0)
                    out[p] = mm(jnp.where(isl, tables[i0], tables[i1]), pair)
                else:
                    out[p] = mm(blk, jnp.concatenate([tables[0][j0], tables[1][j1]], axis=0))
            return carry
        lax.fori_loop(piece * total // pieces, (piece + 1) * total // pieces, step, 0)

    def near_z(k, n):
        products((ni_ref, nj_ref), d_ref, True, "z", wp, pzn, k, n)

    def far_z(k, n):
        products((fi_ref, fj_ref), s_ref, False, "z", wc, pzc, k, n)

    def near_y(k, n):
        products((ni_ref, nj_ref), d_ref, True, "y", (ql, qr), pyn, k, n)

    relay_across()
    relay_along(1, 0, 1)
    relay_along(1, 0, 0)
    relay_w(1)
    answer(0)
    relay_points()
    fill_w(1, wp)
    near_z(0, 2)
    for e in range(1, inner):
        relay_along(1, e, 0)
    near_z(1, 2)
    for d in range(2, deep):
        relay_along(d, 0, 1)
        relay_along(d, 0, 0)
        if d == 2:
            relay_w(0)
            if row_levels > 1:
                answer(1)
            fill_w(0, wc)
        far_z(d - 2, 2 * (deep - 2))
        for e in range(1, inner):
            relay_along(d, e, 0)
        if d == 2:
            fill_p()
    if deep <= 2:
        relay_w(0)
        fill_w(0, wc)
        fill_p()
        far_z(0, 1)
    else:
        far_z(1, 2)
    near_y(0, 1)
    for t in range(2 if deep > 2 else 1, row_levels):
        answer(t)
    for e in range(1, inner):
        for dz in range(deep):
            o = lax.rem(zi + dz, deep) * inner + turn_x(e)
            mail.landed(xpart(o, 1), x_sem.at[o, 1], near_row)

    def fill_x(i, carry):
        o = lax.rem(r + i, rows)
        for m in range(packs):
            split(xc[o, m], xl, xr, 2 * (o * packs + m))
        return carry

    lax.fori_loop(1, rows, fill_x, 0)
    mail.close()


def pick(vals, at):
    out = vals[0]
    for i in range(1, len(vals)):
        out = jnp.where(at == i, vals[i], out)
    return out


def grant(own, operands):
    mib = 1024 * 1024
    return own // mib + 5 if own + operands < 40 * mib else min(62, (own + operands) // mib + 6)


def slot_kernel(rows, cols, unroll, fi_ref, fj_ref, ni_ref, nj_ref, live_ref, xl, xr, pyn, pzn, pzc, s_ref, y_ref, z_ref, n_ref,
                yc, yn, zc, zn, y0, y1):
    _, q, wide = xl.shape
    half = wide // 2
    packs = z_ref.shape[1]
    leaves = 2 * packs
    live = live_ref[0]
    isl = lax.broadcasted_iota(jnp.int32, (q, wide), 1) < half
    lane = lax.broadcasted_iota(jnp.int32, (q, wide), 1)
    none = jnp.zeros((q, wide), BF)
    blank = jnp.zeros((q, wide), F32)

    def clear(acc):
        group = 8
        def step(i, carry):
            for k in range(group):
                acc[i * group + k] = blank
            return carry
        lax.fori_loop(0, acc.shape[0] // group, step, 0)

    for acc in (yc, yn, zc, zn):
        clear(acc)

    def settle(pairs, p, yv, zv, ya, za):
        i0, i1, j0, j1 = place(pairs, p)
        a = ya[i0, :, :half] + yv[:, :half]
        b = ya[i1, :, half:] + yv[:, half:]
        c = za[j0, :, :half] + zv[:, :half]
        d = za[j1, :, half:] + zv[:, half:]
        ya[i0, :, :half] = a
        ya[i1, :, half:] = b
        za[j0, :, :half] = c
        za[j1, :, half:] = d

    def near_step(g, carry):
        for k in range(unroll):
            p = g * unroll + k
            settle((ni_ref, nj_ref), p, pyn[p], pzn[p], yn, zn)
        return carry

    lax.fori_loop(0, ni_ref.shape[1] // (2 * unroll), near_step, 0)

    def far(g, buf):
        for k in range(unroll):
            p = g * unroll + k
            settle((fi_ref, fj_ref), p, buf[k], pzc[p], yc, zc)

    def multiply(g, buf):
        for k in range(unroll):
            p = g * unroll + k
            j0, j1 = fj_ref[0, 2 * p], fj_ref[0, 2 * p + 1]
            blk = s_ref[:, pl.ds(pl.multiple_of(p * wide, wide), wide)]
            reach = jnp.where(2 * p + 1 < live, wide, jnp.where(2 * p < live, half, 0))
            blk = jnp.where(lane < reach, blk, none)
            top = xl[j0]
            bot = xr[j1]
            pair = jnp.concatenate([top, bot], axis=0)
            buf[k] = mm(blk, pair)

    steps = quot(live + 4 * unroll - 1, 4 * unroll)
    multiply(0, y0)
    def step(g, carry):
        multiply(2 * g + 1, y1)
        far(2 * g, y0)
        multiply(2 * g + 2, y0)
        far(2 * g + 1, y1)
        return carry
    lax.fori_loop(0, steps - 1, step, 0)
    multiply(2 * steps - 1, y1)
    far(2 * steps - 2, y0)
    far(2 * steps - 1, y1)

    def fold(acc, at):
        a, b = acc[at], acc[at + 1]
        return (jnp.where(isl, a, b) + pltpu.roll(jnp.where(isl, b, a), half, 1)).astype(BF)

    def out_y(i, carry):
        for kind, acc in enumerate((yc, yn)):
            for m in range(packs):
                y_ref[i, kind, m] = fold(acc, 2 * (i * packs + m))
        return carry

    def out_z(i, carry):
        for m in range(packs):
            z_ref[i, m] = fold(zc, 2 * (i * packs + m))
        return carry

    def out_n(i, carry):
        for m in range(packs):
            n_ref[i, m] = fold(zn, 2 * (i * packs + m))
        return carry

    lax.fori_loop(0, cols, out_y, 0)
    lax.fori_loop(0, rows, out_z, 0)
    lax.fori_loop(0, 3, out_n, 0)


def down_kernel(rows, cols, y_ref, z_ref, n_ref, sib_ref, order_ref, u_ref, v_ref, eu_ref, ev_ref, fu_ref, fv_ref,
                s_ref, o_ref, y_in, z1_in, z1_out, z2_in, zn_in, y_sem, z1_sem, z2_sem, n_sem):
    _, packs, q, wide = z_ref.shape
    half = wide // 2
    deep, inner = grid_of(rows)
    dev_count = rows * cols
    r = lax.axis_index("row")
    c = lax.axis_index("col")
    me = r * cols + c
    zi = r // inner
    xi = lax.rem(r, inner)
    bar = greet(rows, cols, r, c)
    ml, mr = left_mask(half, BF)
    isl = lax.broadcasted_iota(jnp.int32, (q, wide), 1) < half
    hot = one_hot(order_ref, me * order_ref.shape[1])
    eye = twin_eye(half)
    pl.semaphore_wait(bar, rows + cols - 2)
    first = {}
    for d in list(range(1, deep)) + [0]:
        to = lax.rem(zi + d, deep) * inner
        first[d] = []
        for e in range(1, inner):
            peer = lax.rem(xi + e, inner)
            first[d].append(
                push(z_ref.at[to + peer], z1_in.at[d, e - 1], z1_sem, (d, e - 1), "row", zi * inner + peer)
            )
    near = [
        push(n_ref.at[0], zn_in.at[0], n_sem, (0,), "row", lax.rem(r + rows - 1, rows)),
        push(n_ref.at[2], zn_in.at[1], n_sem, (1,), "row", lax.rem(r + 1, rows)),
    ]
    y_copies = []
    for d in range(1, cols):
        peer = lax.rem(c + d, cols)
        y_copies.append(push(y_ref.at[peer], y_in.at[d - 1], y_sem, (d - 1,), "col", peer))

    second = []
    for d in range(1, deep):
        for copy in first[d]:
            copy.wait_recv()
        to = lax.rem(zi + d, deep) * inner + xi
        for m in range(packs):
            total = z_ref[to, m].astype(F32)
            for e in range(inner - 1):
                total = total + z1_in[d, e, m].astype(F32)
            z1_out[d - 1, m] = total.astype(BF)
        second.append(push(z1_out.at[d - 1], z2_in.at[d - 1], z2_sem, (d - 1,), "row", to))

    levels = dev_count.bit_length() - 1
    lane_half = (lax.broadcasted_iota(jnp.int32, (q, wide), 1) >= half).astype(jnp.int32)

    def turned(v, chunk, side):
        return mm2(jnp.where(lane_half == side, v, 0.0), jnp.concatenate([chunk, chunk], axis=0), NT)

    y_down = z_down = None
    for level in range(levels - 1, -1, -1):
        own = me >> level
        side = lax.rem(own, 2)
        sib = sib_ref[level].astype(F32)
        rolled = pltpu.roll(sib, half, 1)
        xs = jnp.where(isl, sib, rolled)
        ws = jnp.where(isl, rolled, 0.0).astype(BF)
        at = dev_count - (dev_count >> level) + own // 2
        cup = chunk_at(s_ref, at, wide)
        dup = jnp.concatenate([cup, cup], axis=0)
        y_term = mm(jnp.where(lane_half == side, xs, 0.0).astype(BF), dup, NT)
        z_raw = jnp.where(lane_half == 1 - side, mm(ws, dup), 0.0)
        z_term = z_raw + pltpu.roll(z_raw, half, 1)
        if level < levels - 1:
            y_term = y_term + turned(y_down, chunk_at(fu_ref, at, wide), side)
            z_term = z_term + turned(z_down, chunk_at(fv_ref, at, wide), side)
        y_down, z_down = y_term, z_term

    perms = []
    for flip, (down, b_ref, e_ref) in enumerate(((y_down, u_ref, eu_ref), (z_down, v_ref, ev_ref))):
        if flip == 0:
            for copy in y_copies:
                copy.wait_recv()
        else:
            for copy in first[0] + second + near:
                copy.wait_recv()
        parts = []
        for m in range(packs):
            cs = slice(m * wide, (m + 1) * wide)
            if flip == 0:
                coef, raw = y_ref[c, 0, m].astype(F32), y_ref[c, 1, m].astype(F32)
                for d in range(cols - 1):
                    coef = coef + y_in[d, 0, m].astype(F32)
                    raw = raw + y_in[d, 1, m].astype(F32)
            else:
                coef, raw = z_ref[r, m].astype(F32), n_ref[1, m].astype(F32)
                for e in range(inner - 1):
                    coef = coef + z1_in[0, e, m].astype(F32)
                for d in range(deep - 1):
                    coef = coef + z2_in[d, m].astype(F32)
                for k in range(2):
                    raw = raw + zn_in[k, m].astype(F32)
            if flip == 0:
                hi, lo = split2(down)
                e = e_ref[:, cs]
                leaf = (coef + mm(e, diag2(hi, ml, mr), NT) + mm(e, diag2(lo, ml, mr), NT)).astype(BF)
                turned = mm(eye, diag2(b_ref[:, cs], ml, mr), NT).astype(BF)
                pts = (mm(turned, diag2(leaf, ml, mr)) + raw).astype(BF)
                parts.append(mm(eye, diag2(pts, ml, mr), NT).astype(BF))
            else:
                leaf = (coef + mm2(down, diag2(e_ref[:, cs], ml, mr), NT)).astype(BF)
                parts.append((mm(leaf, diag2(b_ref[:, cs], ml, mr)) + raw).astype(BF))
        perms.append(jnp.concatenate(parts, axis=1))
    o_ref[...] = mm(jnp.concatenate(perms, axis=0), hot, NT).astype(BF)
    for copies in (*first.values(), second, near, y_copies):
        for copy in copies:
            copy.wait_send()


def per_device(
    x_vectors,
    w_vectors,
    order,
    ubasis,
    vbasis,
    leaf_up_u,
    leaf_up_v,
    coupling,
    coupling_pairs,
    coupling_count,
    near_blocks,
    near_pairs,
    transfer_u,
    transfer_v,
    upper_coupling,
):
    q, piece = x_vectors.shape
    rank = ubasis.shape[0]
    leaves = leaf_up_u.shape[1] // rank
    packs = leaves // 2
    wide = 2 * rank
    rows = lax.axis_size("row")
    cols = lax.axis_size("col")
    deep, inner = grid_of(rows)
    order2 = order.reshape(1, piece)

    def shape(*lead):
        return jax.ShapeDtypeStruct((*lead, q, wide), BF)

    def wide_shape(*lead):
        return jax.ShapeDtypeStruct((*lead, q, wide), F32)

    def buf(*lead, dtype=BF):
        return pltpu.VMEM((*lead, q, wide), dtype)

    def sems(*lead):
        return pltpu.SemaphoreType.DMA((2, *lead))

    def params(mib, cid=None):
        limit = mib * 1024 * 1024
        if cid is None:
            return pltpu.CompilerParams(vmem_limit_bytes=limit)
        return pltpu.CompilerParams(vmem_limit_bytes=limit, collective_id=cid, has_side_effects=True)

    token = pl.pallas_call(
        first_kernel,
        out_shape=jax.ShapeDtypeStruct((1, wide), F32),
        out_specs=VMEM,
        compiler_params=params(1),
        cost_estimate=pl.CostEstimate(flops=2_000_000_000, bytes_accessed=6_000_000, transcendentals=0),
    )()
    loaded = (token, coupling_pairs, near_pairs, order2, x_vectors, w_vectors, vbasis, ubasis, leaf_up_v, leaf_up_u)
    own_x, own_p, own_w, own_n, *spots = pl.pallas_call(
        local_kernel,
        out_shape=(
            shape(packs), shape(packs), shape(2, packs), shape(),
            *(jax.ShapeDtypeStruct((1, v.shape[1]), jnp.int32) for v in (coupling_pairs, coupling_pairs, near_pairs, near_pairs)),
        ),
        in_specs=[VMEM] * 10,
        out_specs=(VMEM,) * 8,
        compiler_params=params(12),
        cost_estimate=pl.CostEstimate(flops=8_000_000, bytes_accessed=20_000, transcendentals=0),
    )(*loaded)
    unroll = UNROLL
    far_pairs = coupling_pairs.shape[1] // 2
    near_pairs_count = near_pairs.shape[1] // 2
    levels = (rows * cols).bit_length() - 1
    row_levels = rows.bit_length() - 1
    tables = 2 * leaves * (3 + cols)
    raw = packs * (rows + 3 + 2 * cols)
    block = q * wide * 2
    x_left, x_right, p_y, p_z, c_z, sibs = pl.pallas_call(
        functools.partial(gather_kernel, rows, cols, 32),
        out_shape=(
            shape(rows * leaves), shape(rows * leaves), wide_shape(near_pairs_count), wide_shape(near_pairs_count),
            wide_shape(far_pairs), shape(levels),
        ),
        in_specs=[SMEM] * 5 + [VMEM] * 8,
        out_specs=(VMEM,) * 6,
        scratch_shapes=[
            buf(rows, packs),
            buf(3, packs),
            buf(cols, 2, packs),
            buf(cols),
            buf(2 * row_levels),
            buf(3 * leaves),
            buf(3 * leaves),
            buf(cols * leaves),
            buf(cols * leaves),
            pltpu.SemaphoreType.DMA((128,)),
            pltpu.SemaphoreType.DMA((rows, 2)),
            pltpu.SemaphoreType.DMA((3,)),
            pltpu.SemaphoreType.DMA((cols, 2)),
            pltpu.SemaphoreType.DMA((cols,)),
            pltpu.SemaphoreType.DMA((row_levels,)),
        ],
        compiler_params=params(6 + (tables + raw) * block // 1024**2, 0),
        cost_estimate=pl.CostEstimate(flops=20_000_000_000, bytes_accessed=60_000_000, transcendentals=0),
    )(
        *spots, coupling_count, own_x, own_p, own_w, own_n, transfer_u, transfer_v,
        coupling, near_blocks,
    )
    sums = leaves * (2 * cols + rows + 3) + 2 * unroll
    y_part, z_part, n_part = pl.pallas_call(
        functools.partial(slot_kernel, rows, cols, unroll),
        out_shape=(shape(cols, 2, packs), shape(rows, packs), shape(3, packs)),
        in_specs=[SMEM] * 5 + [VMEM] * 6,
        out_specs=(VMEM,) * 3,
        scratch_shapes=[
            buf(cols * leaves, dtype=F32),
            buf(cols * leaves, dtype=F32),
            buf(rows * leaves, dtype=F32),
            buf(3 * leaves, dtype=F32),
            buf(unroll, dtype=F32),
            buf(unroll, dtype=F32),
        ],
        compiler_params=params(grant(sums * 2 * block, 2 * rows * leaves * block + (near_pairs_count * 2 + far_pairs) * 2 * block + far_pairs * wide * q * 2)),
        cost_estimate=pl.CostEstimate(flops=20_000_000_000, bytes_accessed=60_000_000, transcendentals=0),
    )(*spots, coupling_count, x_left, x_right, p_y, p_z, c_z, coupling)
    out = pl.pallas_call(
        functools.partial(down_kernel, rows, cols),
        out_shape=jax.ShapeDtypeStruct((2 * q, piece), BF),
        in_specs=[VMEM] * 12,
        out_specs=VMEM,
        scratch_shapes=[
            buf(cols - 1, 2, packs),
            buf(deep, inner - 1, packs),
            buf(deep - 1, packs),
            buf(deep - 1, packs),
            buf(2, packs),
            sems(cols - 1),
            sems(deep, inner - 1),
            sems(deep - 1),
            sems(2),
        ],
        compiler_params=params(16, 1),
    )(
        y_part, z_part, n_part, sibs, order2, ubasis, vbasis, leaf_up_u, leaf_up_v,
        transfer_u, transfer_v, upper_coupling,
    )
    return out[:q], out[q:]


def solution(mesh):
    both = P(None, ("row", "col"))
    flat = P(("row", "col"))
    return jax.shard_map(
        per_device,
        mesh=mesh,
        in_specs=(both, both, flat, both, both, both, both, both, both, flat, both, both, P(), P(), P()),
        out_specs=(both, both),
        check_vma=False,
    )
```

time: 75.1 us -> 68.7 us (0.915)
  Pallas kernels: 71.8 us -> 65.4 us
    pallas_call x1, Pallas kernels: 25.3 us -> 22 us  [per_device(): pl.pallas_call(functools.partial(down_kernel, rows, cols), out_shape=jax....]
    pallas_call x2 -> x3, Pallas kernels: 46.4 us -> 43.4 us  [the longest x1 30.5 us: per_device(): pl.pallas_call(functools.partial(gather_kernel, rows, cols, 32), out_shap...]
where the time goes in v2:
time: 68.7 us
  Pallas kernels  65.4 us (95%)
  local copies, waits for them, and re-layouts  1.73 us (3%)
  between operations  1.62 us (2%)
    pallas_call x1, Pallas kernels, per_device(): pl.pallas_call(functools.partial(gather_kernel, rows, cols, 32), out_shap...  30.5 us
    pallas_call x1, Pallas kernels, per_device(): pl.pallas_call(functools.partial(down_kernel, rows, cols), out_shape=jax....  22 us
    pallas_call x1, Pallas kernels, per_device(): pl.pallas_call(functools.partial(slot_kernel, rows, cols, unroll), out_sh...  11.3 us
    pallas_call x1, Pallas kernels, per_device(): pl.pallas_call(local_kernel, out_shape=(shape(packs), shape(packs), shape...  1.57 us

profile of v2, /device:TPU:0, one launch (start us, length us, event | category | flops | bytes accessed | tf_op | source)
XLA Modules:
  0.0 68.7 jit_solution(3252411190172549646)
XLA Ops:
  0.6 0.0 copy-start.6
  0.6 0.0 copy-start.5
  0.7 0.0 copy-start.12
  0.7 0.0 copy-start.2
  0.7 0.0 copy-start.3
  0.7 0.0 copy-start
  0.7 0.0 copy-start.1
  0.7 0.0 copy-start.11
  0.7 0.0 copy-start.10
  0.7 0.0 copy-start.9
  1.6 0.1 copy-done.2
  1.7 0.1 copy-done.3
  1.8 0.1 copy-done
  1.8 0.1 copy-done.1
  1.9 0.0 copy-done.11
  1.9 0.1 copy-done.8
  2.0 0.0 copy-done.7
  2.0 1.6 %shard_map.159 = (bf16[8,64,128]{2,1,0:T(8,128)(2,1)S(1)}, bf16[8,64,128]{2,1,0:T(8,128)(2,1)S(1)}, bf16[2,8,64,128]{3,2,1,0:T(8,128)(2,1)S(1)}, bf16[64,128]{1,...) custom-call(f32[1,128]{1,0:T(1,128)S(1)} %shard_map.158.token_ref, ...), custom_call_target="tpu_custom_call" | custom-call | flops 8000000 | bytes 20000 | tf_op jit(solution)/shard_map/pallas_call | solution.py:714
  3.6 0.5 copy-done.13
  4.2 30.5 %shard_map.160 = (bf16[128,64,128]{2,1,0:T(8,128)(2,1)S(1)}, bf16[128,64,128]{2,1,0:T(8,128)(2,1)S(1)}, f32[128,64,128]{2,1,0:T(8,128)S(1)}, f32[128,64,128]{2,1...) custom-call(s32[1,512]{1,0:T(1,128)S(1)} %get-tuple-element.19.fi_ref, ...), custom_call_target="tpu_custom_call" | custom-call | flops 20000000000 | bytes 60000000 | tf_op jit(solution)/shard_map/pallas_call | solution.py:733
  34.7 0.0 copy-start.4
  34.7 11.3 %shard_map.161 = (bf16[4,2,8,64,128]{4,3,2,1,0:T(8,128)(2,1)S(1)}, bf16[8,8,64,128]{3,2,1,0:T(8,128)(2,1)S(1)}, bf16[3,8,64,128]{3,2,1,0:T(8,128)(2,1)S(1)}) custom-call(s32[1,512]{1,0:T(1,128)S(1)} %get-tuple-element.19.fi_ref, s32[1,512]{1,0:T(1,128)S(1)} %get-tuple-element.20.fj_ref, s32[1,256]{1,0:T(1,128)S(1)} %get-tuple-element.21.ni_ref, ...), custom_call_target="tpu_custom_call" | custom-call | flops 20000000000 | bytes 60000000 | tf_op jit(solution)/shard_map/pallas_call | solution.py:765
  46.0 22.0 %shard_map.162 = bf16[128,1024]{1,0:T(8,128)(2,1)S(1)} custom-call(bf16[4,2,8,64,128]{4,3,2,1,0:T(8,128)(2,1)S(1)} %get-tuple-element.32.y_ref, bf16[8,8,64,128]{3,2,1,0:T(8,128)(2,1)S(1)} %get-tuple-element.33.z_ref, bf16[3,8,64,128]{3,2,1,0:T(8,128)(2,1)S(1)} %get-tuple-element.34.n_ref, bf16[5,64,128]{2,1,0:T(8,128)(2,1)S(1)} %get-tuple-element.35.sib_ref, ...), custom_call_target="tpu_custom_call" | custom-call | tf_op jit(solution)/shard_map/pallas_call | solution.py:781
  68.0 0.7 %fusion = (bf16[64,1024]{1,0:T(8,128)(2,1)}, bf16[64,1024]{1,0:T(8,128)(2,1)}) fusion(bf16[128,1024]{1,0:T(8,128)(2,1)S(1)} %shard_map.162), kind=kLoop, calls=%fused_computation | loop fusion | bytes 524288 | tf_op jit(solution)/shard_map/slice | solution.py:802
  (10 shorter events, 0.0 us)
Async XLA Ops:
  0.6 3.0 %copy-start.6 = (bf16[64,3840]{1,0:T(8,128)(2,1)S(1)}, bf16[64,3840]{1,0:T(8,128)(2,1)}, u32[]{:S(2)}) copy-start(bf16[64,3840]{1,0:T(8,128)(2,1)} %fv_ref.3) | copy-start | bytes 1474564
  0.6 3.0 %copy-start.5 = (bf16[64,3840]{1,0:T(8,128)(2,1)S(1)}, bf16[64,3840]{1,0:T(8,128)(2,1)}, u32[]{:S(2)}) copy-start(bf16[64,3840]{1,0:T(8,128)(2,1)} %fu_ref.3) | copy-start | bytes 1474564
  0.7 3.0 %copy-start.12 = (bf16[64,32768]{1,0:T(8,128)(2,1)S(1)}, bf16[64,32768]{1,0:T(8,128)(2,1)}, u32[]{:S(2)}) copy-start(bf16[64,32768]{1,0:T(8,128)(2,1)} %s_ref.4) | copy-start | bytes 12582916
  0.7 1.1 %copy-start.2 = (bf16[64,1024]{1,0:T(8,128)(2,1)S(1)}, bf16[64,1024]{1,0:T(8,128)(2,1)}, u32[]{:S(2)}) copy-start(bf16[64,1024]{1,0:T(8,128)(2,1)} %ev_ref.3) | copy-start | bytes 393220
  0.7 1.1 %copy-start.3 = (bf16[64,1024]{1,0:T(8,128)(2,1)S(1)}, bf16[64,1024]{1,0:T(8,128)(2,1)}, u32[]{:S(2)}) copy-start(bf16[64,1024]{1,0:T(8,128)(2,1)} %eu_ref.3) | copy-start | bytes 393220
  0.7 1.2 %copy-start = (bf16[64,1024]{1,0:T(8,128)(2,1)S(1)}, bf16[64,1024]{1,0:T(8,128)(2,1)}, u32[]{:S(2)}) copy-start(bf16[64,1024]{1,0:T(8,128)(2,1)} %v_ref.3) | copy-start | bytes 393220
  0.7 1.2 %copy-start.1 = (bf16[64,1024]{1,0:T(8,128)(2,1)S(1)}, bf16[64,1024]{1,0:T(8,128)(2,1)}, u32[]{:S(2)}) copy-start(bf16[64,1024]{1,0:T(8,128)(2,1)} %u_ref.3) | copy-start | bytes 393220
  0.7 1.2 %copy-start.11 = (s32[2,256]{1,0:T(2,128)S(1)}, s32[2,256]{1,0:T(2,128)}, u32[]{:S(2)}) copy-start(s32[2,256]{1,0:T(2,128)} %near_ref.1) | copy-start | bytes 6148
  0.7 1.2 %copy-start.10 = (s32[2,512]{1,0:T(2,128)S(1)}, s32[2,512]{1,0:T(2,128)}, u32[]{:S(2)}) copy-start(s32[2,512]{1,0:T(2,128)} %far_ref.1) | copy-start | bytes 12292
  0.7 1.2 %copy-start.9 = (s32[1024]{0:T(1024)S(1)}, s32[1024]{0:T(1024)}, u32[]{:S(2)}) copy-start(s32[1024]{0:T(1024)} %param.17) | copy-start | bytes 12292
  0.7 1.3 %copy-start.8 = (bf16[64,1024]{1,0:T(8,128)(2,1)S(1)}, bf16[64,1024]{1,0:T(8,128)(2,1)}, u32[]{:S(2)}) copy-start(bf16[64,1024]{1,0:T(8,128)(2,1)} %w_ref.1) | copy-start | bytes 393220
  0.7 1.3 %copy-start.7 = (bf16[64,1024]{1,0:T(8,128)(2,1)S(1)}, bf16[64,1024]{1,0:T(8,128)(2,1)}, u32[]{:S(2)}) copy-start(bf16[64,1024]{1,0:T(8,128)(2,1)} %x_ref.1) | copy-start | bytes 393220
  0.8 3.4 %copy-start.13 = (bf16[64,16384]{1,0:T(8,128)(2,1)S(1)}, bf16[64,16384]{1,0:T(8,128)(2,1)}, u32[]{:S(2)}) copy-start(bf16[64,16384]{1,0:T(8,128)(2,1)} %d_ref.1) | copy-start | bytes 6291460
  34.7 11.3 %copy-start.4 = (bf16[64,3968]{1,0:T(8,128)(2,1)S(1)}, bf16[64,3968]{1,0:T(8,128)(2,1)}, u32[]{:S(2)}) copy-start(bf16[64,3968]{1,0:T(8,128)(2,1)} %s_ref.5) | copy-start | bytes 1523716

commit v3 on v2

--- a/solution.py
+++ b/solution.py
@@ -193,7 +193,7 @@
     deep, inner = grid_of(rows)
     outer = cols // 2
     dev_count = rows * cols
-    first = (3 * packs) // 8
+    first = (1 * packs) // 8
     cuts = ((0, first), (first, packs - first))
     r = lax.axis_index("row")
     c = lax.axis_index("col")
@@ -387,37 +387,43 @@
     def near_y(k, n):
         products((ni_ref, nj_ref), d_ref, True, "y", (ql, qr), pyn, k, n)
 
+    def fill_rows(e):
+        def step(dz, carry):
+            o = lax.rem(zi + dz, deep) * inner + turn_x(e)
+            for m in range(packs):
+                split(xc[o, m], xl, xr, 2 * (o * packs + m))
+            return carry
+        lax.fori_loop(1 if e == 0 else 0, deep, step, 0)
+
     relay_across()
     relay_along(1, 0, 1)
     relay_along(1, 0, 0)
+    for e in range(1, inner):
+        relay_along(1, e, 0)
     relay_w(1)
     answer(0)
-    relay_points()
     fill_w(1, wp)
-    near_z(0, 2)
-    for e in range(1, inner):
-        relay_along(1, e, 0)
-    near_z(1, 2)
+    near_z(0, 1)
     for d in range(2, deep):
         relay_along(d, 0, 1)
         relay_along(d, 0, 0)
         if d == 2:
+            relay_points()
             relay_w(0)
+        for e in range(1, inner):
+            relay_along(d, e, 0)
+        if d == 2:
             if row_levels > 1:
                 answer(1)
             fill_w(0, wc)
-        far_z(d - 2, 2 * (deep - 2))
-        for e in range(1, inner):
-            relay_along(d, e, 0)
-        if d == 2:
-            fill_p()
+            far_z(0, 1)
     if deep <= 2:
+        relay_points()
         relay_w(0)
         fill_w(0, wc)
-        fill_p()
         far_z(0, 1)
-    else:
-        far_z(1, 2)
+    fill_rows(0)
+    fill_p()
     near_y(0, 1)
     for t in range(2 if deep > 2 else 1, row_levels):
         answer(t)
@@ -425,14 +431,7 @@
         for dz in range(deep):
             o = lax.rem(zi + dz, deep) * inner + turn_x(e)
             mail.landed(xpart(o, 1), x_sem.at[o, 1], near_row)
-
-    def fill_x(i, carry):
-        o = lax.rem(r + i, rows)
-        for m in range(packs):
-            split(xc[o, m], xl, xr, 2 * (o * packs + m))
-        return carry
-
-    lax.fori_loop(1, rows, fill_x, 0)
+        fill_rows(e)
     mail.close()
 
 
@@ -546,7 +545,8 @@
 
 
 def down_kernel(rows, cols, y_ref, z_ref, n_ref, sib_ref, order_ref, u_ref, v_ref, eu_ref, ev_ref, fu_ref, fv_ref,
-                s_ref, o_ref, y_in, z1_in, z1_out, z2_in, zn_in, y_sem, z1_sem, z2_sem, n_sem):
+                s_ref, o_ref, y_in, z1_in, z1_out, z2_in, zn_in, zn_out, ahead_y, ahead_z, u_turn, hot_turn,
+                y_sem, z1_sem, z2_sem, n_sem):
     _, packs, q, wide = z_ref.shape
     half = wide // 2
     deep, inner = grid_of(rows)
@@ -559,9 +559,17 @@
     bar = greet(rows, cols, r, c)
     ml, mr = left_mask(half, BF)
     isl = lax.broadcasted_iota(jnp.int32, (q, wide), 1) < half
-    hot = one_hot(order_ref, me * order_ref.shape[1])
     eye = twin_eye(half)
     pl.semaphore_wait(bar, rows + cols - 2)
+    folded = inner == 2
+    if folded:
+        to = lax.rem(zi + deep - 1 + 2 * xi, deep) * inner + xi
+        near = [push(n_ref.at[2 * xi], zn_in.at[0], n_sem, (0,), "row", to)]
+    else:
+        near = [
+            push(n_ref.at[0], zn_in.at[0], n_sem, (0,), "row", lax.rem(r + rows - 1, rows)),
+            push(n_ref.at[2], zn_in.at[1], n_sem, (1,), "row", lax.rem(r + 1, rows)),
+        ]
     first = {}
     for d in list(range(1, deep)) + [0]:
         to = lax.rem(zi + d, deep) * inner
@@ -571,26 +579,10 @@
             first[d].append(
                 push(z_ref.at[to + peer], z1_in.at[d, e - 1], z1_sem, (d, e - 1), "row", zi * inner + peer)
             )
-    near = [
-        push(n_ref.at[0], zn_in.at[0], n_sem, (0,), "row", lax.rem(r + rows - 1, rows)),
-        push(n_ref.at[2], zn_in.at[1], n_sem, (1,), "row", lax.rem(r + 1, rows)),
-    ]
     y_copies = []
     for d in range(1, cols):
         peer = lax.rem(c + d, cols)
         y_copies.append(push(y_ref.at[peer], y_in.at[d - 1], y_sem, (d - 1,), "col", peer))
-
-    second = []
-    for d in range(1, deep):
-        for copy in first[d]:
-            copy.wait_recv()
-        to = lax.rem(zi + d, deep) * inner + xi
-        for m in range(packs):
-            total = z_ref[to, m].astype(F32)
-            for e in range(inner - 1):
-                total = total + z1_in[d, e, m].astype(F32)
-            z1_out[d - 1, m] = total.astype(BF)
-        second.append(push(z1_out.at[d - 1], z2_in.at[d - 1], z2_sem, (d - 1,), "row", to))
 
     levels = dev_count.bit_length() - 1
     lane_half = (lax.broadcasted_iota(jnp.int32, (q, wide), 1) >= half).astype(jnp.int32)
@@ -617,42 +609,72 @@
             z_term = z_term + turned(z_down, chunk_at(fv_ref, at, wide), side)
         y_down, z_down = y_term, z_term
 
-    perms = []
-    for flip, (down, b_ref, e_ref) in enumerate(((y_down, u_ref, eu_ref), (z_down, v_ref, ev_ref))):
-        if flip == 0:
-            for copy in y_copies:
-                copy.wait_recv()
-        else:
-            for copy in first[0] + second + near:
-                copy.wait_recv()
-        parts = []
+    second = []
+
+    def pass_on(d):
+        for copy in first[d]:
+            copy.wait_recv()
+        to = lax.rem(zi + d, deep) * inner + xi
         for m in range(packs):
-            cs = slice(m * wide, (m + 1) * wide)
-            if flip == 0:
-                coef, raw = y_ref[c, 0, m].astype(F32), y_ref[c, 1, m].astype(F32)
-                for d in range(cols - 1):
-                    coef = coef + y_in[d, 0, m].astype(F32)
-                    raw = raw + y_in[d, 1, m].astype(F32)
-            else:
-                coef, raw = z_ref[r, m].astype(F32), n_ref[1, m].astype(F32)
-                for e in range(inner - 1):
-                    coef = coef + z1_in[0, e, m].astype(F32)
-                for d in range(deep - 1):
-                    coef = coef + z2_in[d, m].astype(F32)
-                for k in range(2):
-                    raw = raw + zn_in[k, m].astype(F32)
-            if flip == 0:
-                hi, lo = split2(down)
-                e = e_ref[:, cs]
-                leaf = (coef + mm(e, diag2(hi, ml, mr), NT) + mm(e, diag2(lo, ml, mr), NT)).astype(BF)
-                turned = mm(eye, diag2(b_ref[:, cs], ml, mr), NT).astype(BF)
-                pts = (mm(turned, diag2(leaf, ml, mr)) + raw).astype(BF)
-                parts.append(mm(eye, diag2(pts, ml, mr), NT).astype(BF))
-            else:
-                leaf = (coef + mm2(down, diag2(e_ref[:, cs], ml, mr), NT)).astype(BF)
-                parts.append((mm(leaf, diag2(b_ref[:, cs], ml, mr)) + raw).astype(BF))
-        perms.append(jnp.concatenate(parts, axis=1))
-    o_ref[...] = mm(jnp.concatenate(perms, axis=0), hot, NT).astype(BF)
+            total = z_ref[to, m].astype(F32)
+            for e in range(inner - 1):
+                total = total + z1_in[d, e, m].astype(F32)
+            z1_out[d - 1, m] = total.astype(BF)
+        second.append(push(z1_out.at[d - 1], z2_in.at[d - 1], z2_sem, (d - 1,), "row", to))
+
+    def pass_near():
+        if folded:
+            near[0].wait_recv()
+            for m in range(packs):
+                zn_out[m] = (zn_in[0, m].astype(F32) + n_ref[2 * (1 - xi), m].astype(F32)).astype(BF)
+            near.append(push(zn_out, zn_in.at[1], n_sem, (1,), "row", zi * inner + 1 - xi))
+
+    def columns(m):
+        return slice(m * wide, (m + 1) * wide)
+
+    if deep > 1:
+        pass_on(1)
+    pass_near()
+    hi, lo = split2(y_down)
+    hi, lo = diag2(hi, ml, mr), diag2(lo, ml, mr)
+    for m in range(packs):
+        e = eu_ref[:, columns(m)]
+        ahead_y[m] = mm(e, hi, NT) + mm(e, lo, NT)
+        ahead_z[m] = mm2(z_down, diag2(ev_ref[:, columns(m)], ml, mr), NT)
+        u_turn[m] = mm(eye, diag2(u_ref[:, columns(m)], ml, mr), NT).astype(BF)
+    if deep > 2:
+        pass_on(2)
+    hot_turn[...] = jnp.transpose(one_hot(order_ref, me * order_ref.shape[1]))
+    for d in range(3, deep):
+        pass_on(d)
+
+    for copy in y_copies:
+        copy.wait_recv()
+    parts = []
+    for m in range(packs):
+        coef, raw = y_ref[c, 0, m].astype(F32), y_ref[c, 1, m].astype(F32)
+        for d in range(cols - 1):
+            coef = coef + y_in[d, 0, m].astype(F32)
+            raw = raw + y_in[d, 1, m].astype(F32)
+        leaf = (coef + ahead_y[m]).astype(BF)
+        pts = (mm(u_turn[m], diag2(leaf, ml, mr)) + raw).astype(BF)
+        parts.append(mm(eye, diag2(pts, ml, mr), NT).astype(BF))
+    o_ref[:q] = mm(jnp.concatenate(parts, axis=1), hot_turn[...]).astype(BF)
+
+    for copy in first[0] + second + near[1 if folded else 0:]:
+        copy.wait_recv()
+    parts = []
+    for m in range(packs):
+        coef, raw = z_ref[r, m].astype(F32), n_ref[1, m].astype(F32)
+        for e in range(inner - 1):
+            coef = coef + z1_in[0, e, m].astype(F32)
+        for d in range(deep - 1):
+            coef = coef + z2_in[d, m].astype(F32)
+        for k in ((1,) if folded else (0, 1)):
+            raw = raw + zn_in[k, m].astype(F32)
+        leaf = (coef + ahead_z[m]).astype(BF)
+        parts.append((mm(leaf, diag2(v_ref[:, columns(m)], ml, mr)) + raw).astype(BF))
+    o_ref[q:] = mm(jnp.concatenate(parts, axis=1), hot_turn[...]).astype(BF)
     for copies in (*first.values(), second, near, y_copies):
         for copy in copies:
             copy.wait_send()
@@ -789,12 +811,17 @@
             buf(deep - 1, packs),
             buf(deep - 1, packs),
             buf(2, packs),
+            buf(packs),
+            buf(packs, dtype=F32),
+            buf(packs, dtype=F32),
+            buf(packs),
+            pltpu.VMEM((piece, piece), BF),
             sems(cols - 1),
             sems(deep, inner - 1),
             sems(deep - 1),
             sems(2),
         ],
-        compiler_params=params(16, 1),
+        compiler_params=params(20, 1),
     )(
         y_part, z_part, n_part, sibs, order2, ubasis, vbasis, leaf_up_u, leaf_up_v,
         transfer_u, transfer_v, upper_coupling,

time: 68.7 us -> 64 us (0.932)
  Pallas kernels: 65.4 us -> 60.9 us
    pallas_call x1, Pallas kernels: 22 us -> 19.2 us  [per_device(): pl.pallas_call(functools.partial(down_kernel, rows, cols), out_shape=jax....]
    pallas_call x1, Pallas kernels: 30.5 us -> 28.9 us  [per_device(): pl.pallas_call(functools.partial(gather_kernel, rows, cols, 32), out_shap...]
where the time goes in v3:
time: 64 us; the launch traced here: 64.3 us
  Pallas kernels  60.9 us (95%)
  local copies, waits for them, and re-layouts  1.73 us (3%)
  between operations  1.62 us (3%)
    pallas_call x1, Pallas kernels, per_device(): pl.pallas_call(functools.partial(gather_kernel, rows, cols, 32), out_shap...  28.9 us
    pallas_call x1, Pallas kernels, per_device(): pl.pallas_call(functools.partial(down_kernel, rows, cols), out_shape=jax....  19.2 us
    pallas_call x1, Pallas kernels, per_device(): pl.pallas_call(functools.partial(slot_kernel, rows, cols, unroll), out_sh...  11.3 us
    pallas_call x1, Pallas kernels, per_device(): pl.pallas_call(local_kernel, out_shape=(shape(packs), shape(packs), shape...  1.57 us

profile of v3, /device:TPU:0, one launch (start us, length us, event | category | flops | bytes accessed | tf_op | source)
XLA Modules:
  0.0 64.3 jit_solution(7812456126182791443)
XLA Ops:
  0.6 0.0 copy-start.6
  0.6 0.0 copy-start.5
  0.7 0.0 copy-start.12
  0.7 0.0 copy-start.2
  0.7 0.0 copy-start.3
  0.7 0.0 copy-start
  0.7 0.0 copy-start.1
  0.7 0.0 copy-start.11
  0.7 0.0 copy-start.10
  0.7 0.0 copy-start.9
  1.6 0.1 copy-done.2
  1.7 0.1 copy-done.3
  1.8 0.1 copy-done
  1.8 0.1 copy-done.1
  1.9 0.0 copy-done.10
  1.9 0.1 copy-done.8
  2.0 0.0 copy-done.7
  2.0 1.6 %shard_map.159 = (bf16[8,64,128]{2,1,0:T(8,128)(2,1)S(1)}, bf16[8,64,128]{2,1,0:T(8,128)(2,1)S(1)}, bf16[2,8,64,128]{3,2,1,0:T(8,128)(2,1)S(1)}, bf16[64,128]{1,...) custom-call(f32[1,128]{1,0:T(1,128)S(1)} %shard_map.158.token_ref, ...), custom_call_target="tpu_custom_call" | custom-call | flops 8000000 | bytes 20000 | tf_op jit(solution)/shard_map/pallas_call | solution.py:736
  3.6 0.5 copy-done.13
  4.2 28.9 %shard_map.160 = (bf16[128,64,128]{2,1,0:T(8,128)(2,1)S(1)}, bf16[128,64,128]{2,1,0:T(8,128)(2,1)S(1)}, f32[128,64,128]{2,1,0:T(8,128)S(1)}, f32[128,64,128]{2,1...) custom-call(s32[1,512]{1,0:T(1,128)S(1)} %get-tuple-element.19.fi_ref, ...), custom_call_target="tpu_custom_call" | custom-call | flops 20000000000 | bytes 60000000 | tf_op jit(solution)/shard_map/pallas_call | solution.py:755
  33.1 0.0 copy-start.4
  33.1 11.3 %shard_map.161 = (bf16[4,2,8,64,128]{4,3,2,1,0:T(8,128)(2,1)S(1)}, bf16[8,8,64,128]{3,2,1,0:T(8,128)(2,1)S(1)}, bf16[3,8,64,128]{3,2,1,0:T(8,128)(2,1)S(1)}) custom-call(s32[1,512]{1,0:T(1,128)S(1)} %get-tuple-element.19.fi_ref, s32[1,512]{1,0:T(1,128)S(1)} %get-tuple-element.20.fj_ref, s32[1,256]{1,0:T(1,128)S(1)} %get-tuple-element.21.ni_ref, ...), custom_call_target="tpu_custom_call" | custom-call | flops 20000000000 | bytes 60000000 | tf_op jit(solution)/shard_map/pallas_call | solution.py:787
  44.4 19.2 %shard_map.162 = bf16[128,1024]{1,0:T(8,128)(2,1)S(1)} custom-call(bf16[4,2,8,64,128]{4,3,2,1,0:T(8,128)(2,1)S(1)} %get-tuple-element.32.y_ref, bf16[8,8,64,128]{3,2,1,0:T(8,128)(2,1)S(1)} %get-tuple-element.33.z_ref, bf16[3,8,64,128]{3,2,1,0:T(8,128)(2,1)S(1)} %get-tuple-element.34.n_ref, bf16[5,64,128]{2,1,0:T(8,128)(2,1)S(1)} %get-tuple-element.35.sib_ref, ...), custom_call_target="tpu_custom_call" | custom-call | tf_op jit(solution)/shard_map/pallas_call | solution.py:803
  63.6 0.7 %fusion = (bf16[64,1024]{1,0:T(8,128)(2,1)}, bf16[64,1024]{1,0:T(8,128)(2,1)}) fusion(bf16[128,1024]{1,0:T(8,128)(2,1)S(1)} %shard_map.162), kind=kLoop, calls=%fused_computation | loop fusion | bytes 524288 | tf_op jit(solution)/shard_map/slice | solution.py:829
  (10 shorter events, 0.0 us)
Async XLA Ops:
  0.6 3.0 %copy-start.6 = (bf16[64,3840]{1,0:T(8,128)(2,1)S(1)}, bf16[64,3840]{1,0:T(8,128)(2,1)}, u32[]{:S(2)}) copy-start(bf16[64,3840]{1,0:T(8,128)(2,1)} %fv_ref.3) | copy-start | bytes 1474564
  0.6 3.0 %copy-start.5 = (bf16[64,3840]{1,0:T(8,128)(2,1)S(1)}, bf16[64,3840]{1,0:T(8,128)(2,1)}, u32[]{:S(2)}) copy-start(bf16[64,3840]{1,0:T(8,128)(2,1)} %fu_ref.3) | copy-start | bytes 1474564
  0.7 3.0 %copy-start.12 = (bf16[64,32768]{1,0:T(8,128)(2,1)S(1)}, bf16[64,32768]{1,0:T(8,128)(2,1)}, u32[]{:S(2)}) copy-start(bf16[64,32768]{1,0:T(8,128)(2,1)} %s_ref.4) | copy-start | bytes 12582916
  0.7 1.1 %copy-start.2 = (bf16[64,1024]{1,0:T(8,128)(2,1)S(1)}, bf16[64,1024]{1,0:T(8,128)(2,1)}, u32[]{:S(2)}) copy-start(bf16[64,1024]{1,0:T(8,128)(2,1)} %ev_ref.3) | copy-start | bytes 393220
  0.7 1.1 %copy-start.3 = (bf16[64,1024]{1,0:T(8,128)(2,1)S(1)}, bf16[64,1024]{1,0:T(8,128)(2,1)}, u32[]{:S(2)}) copy-start(bf16[64,1024]{1,0:T(8,128)(2,1)} %eu_ref.3) | copy-start | bytes 393220
  0.7 1.2 %copy-start = (bf16[64,1024]{1,0:T(8,128)(2,1)S(1)}, bf16[64,1024]{1,0:T(8,128)(2,1)}, u32[]{:S(2)}) copy-start(bf16[64,1024]{1,0:T(8,128)(2,1)} %v_ref.3) | copy-start | bytes 393220
  0.7 1.2 %copy-start.1 = (bf16[64,1024]{1,0:T(8,128)(2,1)S(1)}, bf16[64,1024]{1,0:T(8,128)(2,1)}, u32[]{:S(2)}) copy-start(bf16[64,1024]{1,0:T(8,128)(2,1)} %u_ref.3) | copy-start | bytes 393220
  0.7 1.2 %copy-start.11 = (s32[2,256]{1,0:T(2,128)S(1)}, s32[2,256]{1,0:T(2,128)}, u32[]{:S(2)}) copy-start(s32[2,256]{1,0:T(2,128)} %near_ref.1) | copy-start | bytes 6148
  0.7 1.2 %copy-start.10 = (s32[2,512]{1,0:T(2,128)S(1)}, s32[2,512]{1,0:T(2,128)}, u32[]{:S(2)}) copy-start(s32[2,512]{1,0:T(2,128)} %far_ref.1) | copy-start | bytes 12292
  0.7 1.2 %copy-start.9 = (s32[1024]{0:T(1024)S(1)}, s32[1024]{0:T(1024)}, u32[]{:S(2)}) copy-start(s32[1024]{0:T(1024)} %param.17) | copy-start | bytes 12292
  0.7 1.3 %copy-start.8 = (bf16[64,1024]{1,0:T(8,128)(2,1)S(1)}, bf16[64,1024]{1,0:T(8,128)(2,1)}, u32[]{:S(2)}) copy-start(bf16[64,1024]{1,0:T(8,128)(2,1)} %w_ref.1) | copy-start | bytes 393220
  0.7 1.3 %copy-start.7 = (bf16[64,1024]{1,0:T(8,128)(2,1)S(1)}, bf16[64,1024]{1,0:T(8,128)(2,1)}, u32[]{:S(2)}) copy-start(bf16[64,1024]{1,0:T(8,128)(2,1)} %x_ref.1) | copy-start | bytes 393220
  0.8 3.4 %copy-start.13 = (bf16[64,16384]{1,0:T(8,128)(2,1)S(1)}, bf16[64,16384]{1,0:T(8,128)(2,1)}, u32[]{:S(2)}) copy-start(bf16[64,16384]{1,0:T(8,128)(2,1)} %d_ref.1) | copy-start | bytes 6291460
  33.1 11.3 %copy-start.4 = (bf16[64,3968]{1,0:T(8,128)(2,1)S(1)}, bf16[64,3968]{1,0:T(8,128)(2,1)}, u32[]{:S(2)}) copy-start(bf16[64,3968]{1,0:T(8,128)(2,1)} %s_ref.5) | copy-start | bytes 1523716

commit v4 on v3

--- a/solution.py
+++ b/solution.py
@@ -402,8 +402,9 @@
         relay_along(1, e, 0)
     relay_w(1)
     answer(0)
-    fill_w(1, wp)
-    near_z(0, 1)
+    if deep <= 2:
+        relay_points()
+        relay_w(0)
     for d in range(2, deep):
         relay_along(d, 0, 1)
         relay_along(d, 0, 0)
@@ -415,13 +416,16 @@
         if d == 2:
             if row_levels > 1:
                 answer(1)
+            fill_w(1, wp)
+            near_z(0, 1)
             fill_w(0, wc)
-            far_z(0, 1)
+            far_z(0, 2)
     if deep <= 2:
-        relay_points()
-        relay_w(0)
+        fill_w(1, wp)
+        near_z(0, 1)
         fill_w(0, wc)
-        far_z(0, 1)
+        far_z(0, 2)
+    far_z(1, 2)
     fill_rows(0)
     fill_p()
     near_y(0, 1)

time: 64 us -> 63.7 us (level)
    pallas_call x1, Pallas kernels: 11.3 us -> 6.81 us  [per_device(): pl.pallas_call(functools.partial(slot_kernel, rows, cols, unroll), out_sh...]
    pallas_call x1, Pallas kernels: 19.2 us -> 23 us  [per_device(): pl.pallas_call(functools.partial(down_kernel, rows, cols), out_shape=jax....]
where the time goes in v4:
time: 63.7 us; the launch traced here: 63.6 us
  Pallas kernels  60.3 us (95%)
  local copies, waits for them, and re-layouts  1.73 us (3%)
  between operations  1.62 us (3%)
    pallas_call x1, Pallas kernels, per_device(): pl.pallas_call(functools.partial(gather_kernel, rows, cols, 32), out_shap...  28.9 us
    pallas_call x1, Pallas kernels, per_device(): pl.pallas_call(functools.partial(down_kernel, rows, cols), out_shape=jax....  23 us
    pallas_call x1, Pallas kernels, per_device(): pl.pallas_call(functools.partial(slot_kernel, rows, cols, unroll), out_sh...  6.81 us
    pallas_call x1, Pallas kernels, per_device(): pl.pallas_call(local_kernel, out_shape=(shape(packs), shape(packs), shape...  1.57 us

profile of v4, /device:TPU:0, one launch (start us, length us, event | category | flops | bytes accessed | tf_op | source)
XLA Modules:
  0.0 63.6 jit_solution(4148751249970426471)
XLA Ops:
  0.6 0.0 copy-start.6
  0.6 0.0 copy-start.5
  0.7 0.0 copy-start.12
  0.7 0.0 copy-start.2
  0.7 0.0 copy-start.3
  0.7 0.0 copy-start
  0.7 0.0 copy-start.1
  0.7 0.0 copy-start.11
  0.7 0.0 copy-start.10
  0.7 0.0 copy-start.9
  0.7 0.0 copy-start.8
  1.6 0.1 copy-done.2
  1.7 0.1 copy-done.3
  1.8 0.1 copy-done
  1.8 0.1 copy-done.1
  1.9 0.1 copy-done.8
  2.0 0.0 copy-done.7
  2.0 1.6 %shard_map.159 = (bf16[8,64,128]{2,1,0:T(8,128)(2,1)S(1)}, bf16[8,64,128]{2,1,0:T(8,128)(2,1)S(1)}, bf16[2,8,64,128]{3,2,1,0:T(8,128)(2,1)S(1)}, bf16[64,128]{1,...) custom-call(f32[1,128]{1,0:T(1,128)S(1)} %shard_map.158.token_ref, ...), custom_call_target="tpu_custom_call" | custom-call | flops 8000000 | bytes 20000 | tf_op jit(solution)/shard_map/pallas_call | solution.py:740
  3.6 0.5 copy-done.13
  4.2 28.9 %shard_map.160 = (bf16[128,64,128]{2,1,0:T(8,128)(2,1)S(1)}, bf16[128,64,128]{2,1,0:T(8,128)(2,1)S(1)}, f32[128,64,128]{2,1,0:T(8,128)S(1)}, f32[128,64,128]{2,1...) custom-call(s32[1,512]{1,0:T(1,128)S(1)} %get-tuple-element.19.fi_ref, ...), custom_call_target="tpu_custom_call" | custom-call | flops 20000000000 | bytes 60000000 | tf_op jit(solution)/shard_map/pallas_call | solution.py:759
  33.0 0.0 copy-start.4
  33.1 6.8 %shard_map.161 = (bf16[4,2,8,64,128]{4,3,2,1,0:T(8,128)(2,1)S(1)}, bf16[8,8,64,128]{3,2,1,0:T(8,128)(2,1)S(1)}, bf16[3,8,64,128]{3,2,1,0:T(8,128)(2,1)S(1)}) custom-call(s32[1,512]{1,0:T(1,128)S(1)} %get-tuple-element.19.fi_ref, s32[1,512]{1,0:T(1,128)S(1)} %get-tuple-element.20.fj_ref, s32[1,256]{1,0:T(1,128)S(1)} %get-tuple-element.21.ni_ref, ...), custom_call_target="tpu_custom_call" | custom-call | flops 20000000000 | bytes 60000000 | tf_op jit(solution)/shard_map/pallas_call | solution.py:791
  39.9 23.0 %shard_map.162 = bf16[128,1024]{1,0:T(8,128)(2,1)S(1)} custom-call(bf16[4,2,8,64,128]{4,3,2,1,0:T(8,128)(2,1)S(1)} %get-tuple-element.32.y_ref, bf16[8,8,64,128]{3,2,1,0:T(8,128)(2,1)S(1)} %get-tuple-element.33.z_ref, bf16[3,8,64,128]{3,2,1,0:T(8,128)(2,1)S(1)} %get-tuple-element.34.n_ref, bf16[5,64,128]{2,1,0:T(8,128)(2,1)S(1)} %get-tuple-element.35.sib_ref, ...), custom_call_target="tpu_custom_call" | custom-call | tf_op jit(solution)/shard_map/pallas_call | solution.py:807
  62.9 0.7 %fusion = (bf16[64,1024]{1,0:T(8,128)(2,1)}, bf16[64,1024]{1,0:T(8,128)(2,1)}) fusion(bf16[128,1024]{1,0:T(8,128)(2,1)S(1)} %shard_map.162), kind=kLoop, calls=%fused_computation | loop fusion | bytes 524288 | tf_op jit(solution)/shard_map/slice | solution.py:833
  (10 shorter events, 0.0 us)
Async XLA Ops:
  0.6 3.0 %copy-start.6 = (bf16[64,3840]{1,0:T(8,128)(2,1)S(1)}, bf16[64,3840]{1,0:T(8,128)(2,1)}, u32[]{:S(2)}) copy-start(bf16[64,3840]{1,0:T(8,128)(2,1)} %fv_ref.3) | copy-start | bytes 1474564
  0.6 3.0 %copy-start.5 = (bf16[64,3840]{1,0:T(8,128)(2,1)S(1)}, bf16[64,3840]{1,0:T(8,128)(2,1)}, u32[]{:S(2)}) copy-start(bf16[64,3840]{1,0:T(8,128)(2,1)} %fu_ref.3) | copy-start | bytes 1474564
  0.7 3.0 %copy-start.12 = (bf16[64,32768]{1,0:T(8,128)(2,1)S(1)}, bf16[64,32768]{1,0:T(8,128)(2,1)}, u32[]{:S(2)}) copy-start(bf16[64,32768]{1,0:T(8,128)(2,1)} %s_ref.4) | copy-start | bytes 12582916
  0.7 1.1 %copy-start.2 = (bf16[64,1024]{1,0:T(8,128)(2,1)S(1)}, bf16[64,1024]{1,0:T(8,128)(2,1)}, u32[]{:S(2)}) copy-start(bf16[64,1024]{1,0:T(8,128)(2,1)} %ev_ref.3) | copy-start | bytes 393220
  0.7 1.1 %copy-start.3 = (bf16[64,1024]{1,0:T(8,128)(2,1)S(1)}, bf16[64,1024]{1,0:T(8,128)(2,1)}, u32[]{:S(2)}) copy-start(bf16[64,1024]{1,0:T(8,128)(2,1)} %eu_ref.3) | copy-start | bytes 393220
  0.7 1.2 %copy-start = (bf16[64,1024]{1,0:T(8,128)(2,1)S(1)}, bf16[64,1024]{1,0:T(8,128)(2,1)}, u32[]{:S(2)}) copy-start(bf16[64,1024]{1,0:T(8,128)(2,1)} %v_ref.3) | copy-start | bytes 393220
  0.7 1.2 %copy-start.1 = (bf16[64,1024]{1,0:T(8,128)(2,1)S(1)}, bf16[64,1024]{1,0:T(8,128)(2,1)}, u32[]{:S(2)}) copy-start(bf16[64,1024]{1,0:T(8,128)(2,1)} %u_ref.3) | copy-start | bytes 393220
  0.7 1.2 %copy-start.11 = (s32[2,256]{1,0:T(2,128)S(1)}, s32[2,256]{1,0:T(2,128)}, u32[]{:S(2)}) copy-start(s32[2,256]{1,0:T(2,128)} %near_ref.1) | copy-start | bytes 6148
  0.7 1.2 %copy-start.10 = (s32[2,512]{1,0:T(2,128)S(1)}, s32[2,512]{1,0:T(2,128)}, u32[]{:S(2)}) copy-start(s32[2,512]{1,0:T(2,128)} %far_ref.1) | copy-start | bytes 12292
  0.7 1.2 %copy-start.9 = (s32[1024]{0:T(1024)S(1)}, s32[1024]{0:T(1024)}, u32[]{:S(2)}) copy-start(s32[1024]{0:T(1024)} %param.17) | copy-start | bytes 12292
  0.7 1.3 %copy-start.8 = (bf16[64,1024]{1,0:T(8,128)(2,1)S(1)}, bf16[64,1024]{1,0:T(8,128)(2,1)}, u32[]{:S(2)}) copy-start(bf16[64,1024]{1,0:T(8,128)(2,1)} %w_ref.1) | copy-start | bytes 393220
  0.7 1.3 %copy-start.7 = (bf16[64,1024]{1,0:T(8,128)(2,1)S(1)}, bf16[64,1024]{1,0:T(8,128)(2,1)}, u32[]{:S(2)}) copy-start(bf16[64,1024]{1,0:T(8,128)(2,1)} %x_ref.1) | copy-start | bytes 393220
  0.8 3.4 %copy-start.13 = (bf16[64,16384]{1,0:T(8,128)(2,1)S(1)}, bf16[64,16384]{1,0:T(8,128)(2,1)}, u32[]{:S(2)}) copy-start(bf16[64,16384]{1,0:T(8,128)(2,1)} %d_ref.1) | copy-start | bytes 6291460
  33.0 6.8 %copy-start.4 = (bf16[64,3968]{1,0:T(8,128)(2,1)S(1)}, bf16[64,3968]{1,0:T(8,128)(2,1)}, u32[]{:S(2)}) copy-start(bf16[64,3968]{1,0:T(8,128)(2,1)} %s_ref.5) | copy-start | bytes 1523716

commit v5 on v4

--- a/solution.py
+++ b/solution.py
@@ -13,7 +13,7 @@
 SMEM = pl.BlockSpec(memory_space=pltpu.SMEM)
 NN = (((1,), (0,)), ((), ()))
 NT = (((1,), (1,)), ((), ()))
-UNROLL = 8
+UNROLL = 16
 
 
 def mm(a, b, dims=NN):
@@ -528,9 +528,13 @@
         return (jnp.where(isl, a, b) + pltpu.roll(jnp.where(isl, b, a), half, 1)).astype(BF)
 
     def out_y(i, carry):
-        for kind, acc in enumerate((yc, yn)):
-            for m in range(packs):
-                y_ref[i, kind, m] = fold(acc, 2 * (i * packs + m))
+        for m in range(packs):
+            y_ref[i, 0, m] = fold(yc, 2 * (i * packs + m))
+        return carry
+
+    def out_p(i, carry):
+        for m in range(packs):
+            y_ref[i, 1, m] = fold(yn, 2 * (i * packs + m))
         return carry
 
     def out_z(i, carry):
@@ -544,6 +548,7 @@
         return carry
 
     lax.fori_loop(0, cols, out_y, 0)
+    lax.fori_loop(0, cols, out_p, 0)
     lax.fori_loop(0, rows, out_z, 0)
     lax.fori_loop(0, 3, out_n, 0)
 

time: 63.7 us -> 63.6 us (level)
    pallas_call x1, Pallas kernels: 6.81 us -> 8.33 us  [per_device(): pl.pallas_call(functools.partial(slot_kernel, rows, cols, unroll), out_sh...]
    pallas_call x1, Pallas kernels: 23 us -> 21.6 us  [per_device(): pl.pallas_call(functools.partial(down_kernel, rows, cols), out_shape=jax....]
where the time goes in v5:
time: 63.6 us; the launch traced here: 63.7 us
  Pallas kernels  60.4 us (95%)
  local copies, waits for them, and re-layouts  1.73 us (3%)
  between operations  1.62 us (3%)
    pallas_call x1, Pallas kernels, per_device(): pl.pallas_call(functools.partial(gather_kernel, rows, cols, 32), out_shap...  28.9 us
    pallas_call x1, Pallas kernels, per_device(): pl.pallas_call(functools.partial(down_kernel, rows, cols), out_shape=jax....  21.6 us
    pallas_call x1, Pallas kernels, per_device(): pl.pallas_call(functools.partial(slot_kernel, rows, cols, unroll), out_sh...  8.33 us
    pallas_call x1, Pallas kernels, per_device(): pl.pallas_call(local_kernel, out_shape=(shape(packs), shape(packs), shape...  1.57 us

profile of v5, /device:TPU:0, one launch (start us, length us, event | category | flops | bytes accessed | tf_op | source)
XLA Modules:
  0.0 63.7 jit_solution(12384389786108894540)
XLA Ops:
  0.6 0.0 copy-start.6
  0.6 0.0 copy-start.5
  0.7 0.0 copy-start.12
  0.7 0.0 copy-start.2
  0.7 0.0 copy-start.3
  0.7 0.0 copy-start
  0.7 0.0 copy-start.1
  0.7 0.0 copy-start.11
  0.7 0.0 copy-start.10
  0.7 0.0 copy-start.9
  0.7 0.0 copy-start.8
  1.6 0.1 copy-done.2
  1.7 0.1 copy-done.3
  1.8 0.1 copy-done
  1.8 0.1 copy-done.1
  1.9 0.1 copy-done.8
  2.0 0.0 copy-done.7
  2.0 1.6 %shard_map.159 = (bf16[8,64,128]{2,1,0:T(8,128)(2,1)S(1)}, bf16[8,64,128]{2,1,0:T(8,128)(2,1)S(1)}, bf16[2,8,64,128]{3,2,1,0:T(8,128)(2,1)S(1)}, bf16[64,128]{1,...) custom-call(f32[1,128]{1,0:T(1,128)S(1)} %shard_map.158.token_ref, ...), custom_call_target="tpu_custom_call" | custom-call | flops 8000000 | bytes 20000 | tf_op jit(solution)/shard_map/pallas_call | solution.py:745
  3.6 0.5 copy-done.13
  4.2 28.9 %shard_map.160 = (bf16[128,64,128]{2,1,0:T(8,128)(2,1)S(1)}, bf16[128,64,128]{2,1,0:T(8,128)(2,1)S(1)}, f32[128,64,128]{2,1,0:T(8,128)S(1)}, f32[128,64,128]{2,1...) custom-call(s32[1,512]{1,0:T(1,128)S(1)} %get-tuple-element.19.fi_ref, ...), custom_call_target="tpu_custom_call" | custom-call | flops 20000000000 | bytes 60000000 | tf_op jit(solution)/shard_map/pallas_call | solution.py:764
  33.0 0.0 copy-start.4
  33.1 8.3 %shard_map.161 = (bf16[4,2,8,64,128]{4,3,2,1,0:T(8,128)(2,1)S(1)}, bf16[8,8,64,128]{3,2,1,0:T(8,128)(2,1)S(1)}, bf16[3,8,64,128]{3,2,1,0:T(8,128)(2,1)S(1)}) custom-call(s32[1,512]{1,0:T(1,128)S(1)} %get-tuple-element.19.fi_ref, s32[1,512]{1,0:T(1,128)S(1)} %get-tuple-element.20.fj_ref, s32[1,256]{1,0:T(1,128)S(1)} %get-tuple-element.21.ni_ref, ...), custom_call_target="tpu_custom_call" | custom-call | flops 20000000000 | bytes 60000000 | tf_op jit(solution)/shard_map/pallas_call | solution.py:796
  41.4 21.6 %shard_map.162 = bf16[128,1024]{1,0:T(8,128)(2,1)S(1)} custom-call(bf16[4,2,8,64,128]{4,3,2,1,0:T(8,128)(2,1)S(1)} %get-tuple-element.32.y_ref, bf16[8,8,64,128]{3,2,1,0:T(8,128)(2,1)S(1)} %get-tuple-element.33.z_ref, bf16[3,8,64,128]{3,2,1,0:T(8,128)(2,1)S(1)} %get-tuple-element.34.n_ref, bf16[5,64,128]{2,1,0:T(8,128)(2,1)S(1)} %get-tuple-element.35.sib_ref, ...), custom_call_target="tpu_custom_call" | custom-call | tf_op jit(solution)/shard_map/pallas_call | solution.py:812
  63.0 0.7 %fusion = (bf16[64,1024]{1,0:T(8,128)(2,1)}, bf16[64,1024]{1,0:T(8,128)(2,1)}) fusion(bf16[128,1024]{1,0:T(8,128)(2,1)S(1)} %shard_map.162), kind=kLoop, calls=%fused_computation | loop fusion | bytes 524288 | tf_op jit(solution)/shard_map/slice | solution.py:838
  (10 shorter events, 0.0 us)
Async XLA Ops:
  0.6 3.0 %copy-start.6 = (bf16[64,3840]{1,0:T(8,128)(2,1)S(1)}, bf16[64,3840]{1,0:T(8,128)(2,1)}, u32[]{:S(2)}) copy-start(bf16[64,3840]{1,0:T(8,128)(2,1)} %fv_ref.3) | copy-start | bytes 1474564
  0.6 3.0 %copy-start.5 = (bf16[64,3840]{1,0:T(8,128)(2,1)S(1)}, bf16[64,3840]{1,0:T(8,128)(2,1)}, u32[]{:S(2)}) copy-start(bf16[64,3840]{1,0:T(8,128)(2,1)} %fu_ref.3) | copy-start | bytes 1474564
  0.7 3.0 %copy-start.12 = (bf16[64,32768]{1,0:T(8,128)(2,1)S(1)}, bf16[64,32768]{1,0:T(8,128)(2,1)}, u32[]{:S(2)}) copy-start(bf16[64,32768]{1,0:T(8,128)(2,1)} %s_ref.4) | copy-start | bytes 12582916
  0.7 1.1 %copy-start.2 = (bf16[64,1024]{1,0:T(8,128)(2,1)S(1)}, bf16[64,1024]{1,0:T(8,128)(2,1)}, u32[]{:S(2)}) copy-start(bf16[64,1024]{1,0:T(8,128)(2,1)} %ev_ref.3) | copy-start | bytes 393220
  0.7 1.1 %copy-start.3 = (bf16[64,1024]{1,0:T(8,128)(2,1)S(1)}, bf16[64,1024]{1,0:T(8,128)(2,1)}, u32[]{:S(2)}) copy-start(bf16[64,1024]{1,0:T(8,128)(2,1)} %eu_ref.3) | copy-start | bytes 393220
  0.7 1.2 %copy-start = (bf16[64,1024]{1,0:T(8,128)(2,1)S(1)}, bf16[64,1024]{1,0:T(8,128)(2,1)}, u32[]{:S(2)}) copy-start(bf16[64,1024]{1,0:T(8,128)(2,1)} %v_ref.3) | copy-start | bytes 393220
  0.7 1.2 %copy-start.1 = (bf16[64,1024]{1,0:T(8,128)(2,1)S(1)}, bf16[64,1024]{1,0:T(8,128)(2,1)}, u32[]{:S(2)}) copy-start(bf16[64,1024]{1,0:T(8,128)(2,1)} %u_ref.3) | copy-start | bytes 393220
  0.7 1.2 %copy-start.11 = (s32[2,256]{1,0:T(2,128)S(1)}, s32[2,256]{1,0:T(2,128)}, u32[]{:S(2)}) copy-start(s32[2,256]{1,0:T(2,128)} %near_ref.1) | copy-start | bytes 6148
  0.7 1.2 %copy-start.10 = (s32[2,512]{1,0:T(2,128)S(1)}, s32[2,512]{1,0:T(2,128)}, u32[]{:S(2)}) copy-start(s32[2,512]{1,0:T(2,128)} %far_ref.1) | copy-start | bytes 12292
  0.7 1.2 %copy-start.9 = (s32[1024]{0:T(1024)S(1)}, s32[1024]{0:T(1024)}, u32[]{:S(2)}) copy-start(s32[1024]{0:T(1024)} %param.17) | copy-start | bytes 12292
  0.7 1.3 %copy-start.8 = (bf16[64,1024]{1,0:T(8,128)(2,1)S(1)}, bf16[64,1024]{1,0:T(8,128)(2,1)}, u32[]{:S(2)}) copy-start(bf16[64,1024]{1,0:T(8,128)(2,1)} %w_ref.1) | copy-start | bytes 393220
  0.7 1.3 %copy-start.7 = (bf16[64,1024]{1,0:T(8,128)(2,1)S(1)}, bf16[64,1024]{1,0:T(8,128)(2,1)}, u32[]{:S(2)}) copy-start(bf16[64,1024]{1,0:T(8,128)(2,1)} %x_ref.1) | copy-start | bytes 393220
  0.8 3.4 %copy-start.13 = (bf16[64,16384]{1,0:T(8,128)(2,1)S(1)}, bf16[64,16384]{1,0:T(8,128)(2,1)}, u32[]{:S(2)}) copy-start(bf16[64,16384]{1,0:T(8,128)(2,1)} %d_ref.1) | copy-start | bytes 6291460
  33.0 8.4 %copy-start.4 = (bf16[64,3968]{1,0:T(8,128)(2,1)S(1)}, bf16[64,3968]{1,0:T(8,128)(2,1)}, u32[]{:S(2)}) copy-start(bf16[64,3968]{1,0:T(8,128)(2,1)} %s_ref.5) | copy-start | bytes 1523716
